TPU v7x, 32 devices: a whole 2x2x4 slice. The times are simulated.
32 devices in a mesh: rows: 16 (over z, y, x), cols: 2 (over core).
Axes of the slice: x: 2, y: 2, z: 4, core: 2. Of those that a mesh axis runs over, the one named last changes fastest.
Arguments:
- descriptors: bfloat16 [4096, 1024], P(('rows', 'cols')), may hold values from -6 to 6
- sparse_points: bfloat16 [8192, 1024], P('cols'), may hold values from -6 to 6
- point_scale: float32 [8192], P('cols'), may hold values from 0.3 to 3
- env_owner: int32 [4096, 1], P('rows'), may hold values from 0 to 15; in each aligned block of 128 rows (0 to 127, 128 to 255, ...) at most 12 rows name the same one
- env_structure: int32 [4096], P('rows'), may hold values from 0 to 63
- row_weight: float32 [1024], P('rows'), may hold values from 0.01 to 0.1
- ridge_factor: float32 [1], replicated, may hold values from 0.05 to 0.5
Outputs:
- r_rows: float32 [128, 8192], P(None, 'cols')
- reduced: float32 [1024, 8192], P('rows', 'cols')
Inputs may be any that keep to these rules, and one draw needn't show every extreme that they name: `env_owner`: in each aligned block of 128 environments, no owner is named by more than 12 of them.
All inputs are finite; a program needn't handle non-finite values.
Results may differ from a plain program's by a relative error of at most 0.0045.
Values may be sent and summed in bfloat16 or wider, within the bound.
A program may use at most 64 MiB of HBM per device.

v0:
```python
import math

import jax
import jax.numpy as jnp
from jax import lax
from jax.sharding import PartitionSpec as P

PW = 64
PANELS = 2
BLOCK = 128
LANES = 128
HI = lax.Precision.HIGHEST
F32 = jnp.float32


def mm(left, right, contract, precision=HI):
    return lax.dot_general(
        left, right, ((contract[0], contract[1]), ((), ())), precision=precision,
        preferred_element_type=F32,
    )


def from_root(value, axis):
    return lax.all_gather(value, axis)[0]


def kernel_rows(env_rows, points, scale):
    products = mm(env_rows, points, ((1,), (1,)), None) * env_rows.shape[1] ** (-0.5)
    squared = products * products
    return (scale[None, :] * squared * squared).astype(jnp.bfloat16)


def spread(value, axis):
    size = lax.axis_size(axis)
    return lax.all_to_all(
        jnp.broadcast_to(value[None], (size,) + value.shape), axis, 0, 0, tiled=True
    )


def factor(gram_mat, ridge_factor):
    eye = jnp.eye(PW, dtype=F32)
    shift = ridge_factor[0] * jnp.trace(gram_mat) / PW + 1e-06
    chol_lower = jnp.linalg.cholesky(gram_mat + shift * eye)
    return chol_lower, jax.scipy.linalg.solve_triangular(chol_lower, eye, lower=True)


def body(
    descriptors, sparse_points, point_scale, env_owner, env_structure, row_weight, ridge_factor
):
    owners = lax.axis_size("rows")
    col_index = lax.axis_index("cols")
    eq_count = row_weight.shape[0]
    env_local, desc = descriptors.shape
    wide = PANELS * PW

    head_points = from_root(sparse_points[:wide], "cols")
    head_scale = from_root(point_scale[:wide], "cols")

    per_block = max(2, (3 * BLOCK + 2 * owners - 1) // (2 * owners))
    capacity = min(env_local, per_block * (-(-env_local // BLOCK)))
    own = lax.dynamic_slice_in_dim(env_owner[:, 0], col_index * env_local, env_local)
    struct = lax.dynamic_slice_in_dim(env_structure, col_index * env_local, env_local)
    idx = jnp.arange(env_local)
    within = jnp.sum(
        ((own[:, None] == own[None, :]) & (idx[None, :] < idx[:, None])).astype(jnp.int32), axis=1
    )
    slot = own * capacity + within
    slots = lax.broadcasted_iota(jnp.int32, (owners * capacity, env_local), 0)
    pick = (slots == slot[None, :]).astype(jnp.bfloat16)
    lane = lax.broadcasted_iota(jnp.int32, (env_local, LANES), 1)
    tag = jnp.where(lane == 0, struct[:, None] + 1, 0).astype(jnp.bfloat16)
    payload = mm(
        pick, jnp.concatenate([descriptors, tag], axis=1), ((1,), (0,)), None
    ).astype(jnp.bfloat16)
    arrived = lax.all_to_all(payload, "rows", 0, 0, tiled=True)
    arrived = lax.all_gather(arrived, "cols", axis=0, tiled=True)
    env_rows = arrived[:, :desc]
    labels = arrived[:, desc].astype(jnp.int32) - 1
    targets = lax.broadcasted_iota(jnp.int32, (eq_count, labels.shape[0]), 0)
    selector = (labels[None, :] == targets).astype(jnp.bfloat16)

    def equations(points, scale):
        kernel = kernel_rows(env_rows, points, scale)
        return mm(selector, kernel, ((1,), (0,)), None) * row_weight[:, None]

    head = equations(head_points, head_scale)
    head_all = spread(head, "rows").reshape(owners * eq_count, wide)
    matrix = equations(sparse_points, point_scale)
    col_count = matrix.shape[1]

    part = col_count // owners
    cross = mm(head, matrix, ((0,), (0,)))
    cross = cross.reshape(wide, owners, part).transpose(1, 0, 2).astype(jnp.bfloat16)
    cross = lax.all_to_all(cross, "rows", 0, 0, tiled=True)
    cross = jnp.sum(cross.astype(F32), axis=0)

    gram = mm(head_all, head_all, ((0,), (0,)))
    low1, inv1 = factor(gram[:PW, :PW], ridge_factor)
    c12 = mm(inv1, gram[:PW, PW:], ((1,), (0,)))
    overlap = mm(mm(inv1, gram[:PW, :PW], ((1,), (0,))), inv1, ((1,), (1,)))
    twice = 2.0 * jnp.eye(PW, dtype=F32) - overlap
    mixed = mm(c12, twice, ((0,), (0,)))
    low2, inv2 = factor(gram[PW:, PW:] - mm(mixed, c12, ((1,), (0,))), ridge_factor)
    q1 = mm(head[:, :PW], inv1, ((1,), (1,)))
    q2 = mm(head[:, PW:] - mm(q1, c12, ((1,), (0,))), inv2, ((1,), (1,)))

    c1 = mm(inv1, cross[:PW], ((1,), (0,)))
    c2 = mm(inv2, cross[PW:] - mm(mixed, c1, ((1,), (0,))), ((1,), (0,)))
    coupled = spread(jnp.concatenate([c1, c2], axis=0).astype(jnp.bfloat16), "rows")
    coupled = coupled.transpose(1, 0, 2).reshape(wide, col_count).astype(F32)

    q_cols = jnp.concatenate([q1, q2], axis=1)
    update = mm(q_cols, coupled, ((1,), (0,)))
    norm_scale = 1.0 / math.sqrt(owners * eq_count)
    zero = jnp.zeros((PW, PW), F32)
    r_head = jnp.concatenate(
        [jnp.concatenate([low1.T, c12], axis=1), jnp.concatenate([zero, low2.T], axis=1)], axis=0
    )
    root = col_index == 0
    reduced = matrix - update
    reduced_head = jnp.where(root, q_cols, reduced[:, :wide])
    r_head = jnp.where(root, r_head, coupled[:, :wide])
    reduced = jnp.concatenate([reduced_head, reduced[:, wide:]], axis=1)
    r_rows = jnp.concatenate([r_head, coupled[:, wide:]], axis=1) * norm_scale
    return r_rows, reduced


def solution(mesh):
    return jax.shard_map(
        body,
        mesh=mesh,
        in_specs=(
            P(("rows", "cols"), None),
            P("cols", None),
            P("cols"),
            P("rows", None),
            P("rows"),
            P("rows"),
            P(),
        ),
        out_specs=(P(None, "cols"), P("rows", "cols")),
        check_vma=False,
    )
```

profile of v0, /device:TPU:0, one launch (start us, length us, event | category | flops | bytes accessed | tf_op | source)
XLA Modules:
  0.0 124.6 jit_solution(13761255748347640097)
XLA Ops:
  0.7 0.8 dynamic-slice_add_fusion
  1.5 0.7 dynamic-slice_bitcast_fusion
  2.1 0.2 convert_reduce_fusion.1
  2.3 0.7 multiply_add_fusion
  3.0 0.1 select_convert_fusion
  3.1 1.2 convolution_convert_fusion.1
  4.3 0.9 all_to_all.17
  5.2 8.3 %all-to-all-start = ((bf16[16,12,1152]{2,1,0:T(8,128)(2,1)}), bf16[16,12,1152]{2,1,0:T(8,128)(2,1)S(1)}, u32[]{:S(2)}, u32[]{:S(2)}) async-start(bf16[16,12,1152]{2,1,0:T(8,128)(2,1)} %all_to_all.17), calls=%async_computation | async-start | bytes 1179648 | tf_op jit(solution)/shard_map/all_to_all | solution.py:75
  14.2 1.8 %all-gather.2 = f32[2,1,128]{2,1,0:T(1,128)S(1)} all-gather(f32[1,1,128]{2,1,0:T(1,128)S(1)} %slice_bitcast_fusion.1), channel_id=2, replica_groups=mesh['rows'=16,'cols'=2] {'cols'}, dimensions={0}, use_global_device_ids=true | all-gather | bytes 1536 | tf_op jit(solution)/shard_map/all_gather | solution.py:24
  16.0 2.2 %all-gather.1 = bf16[256,1024]{1,0:T(8,128)(2,1)S(1)} all-gather(bf16[128,1024]{1,0:T(8,128)(2,1)S(1)} %slice-done.1), channel_id=3, replica_groups=mesh['rows'=16,'cols'=2] {'cols'}, dimensions={0}, use_global_device_ids=true | all-gather | bytes 786432 | tf_op jit(solution)/shard_map/all_gather | solution.py:24
  18.2 11.6 %all-to-all-done = bf16[16,12,1152]{2,1,0:T(8,128)(2,1)S(1)} async-done(((bf16[16,12,1152]{2,1,0:T(8,128)(2,1)}), bf16[16,12,1152]{2,1,0:T(8,128)(2,1)S(1)}, u32[]{:S(2)}, u32[]{:S(2)}) %all-to-all-start) | async-done | bytes 442400 | tf_op jit(solution)/shard_map/all_to_all | solution.py:75
  29.8 0.1 all_to_all.19
  29.9 2.4 %all_gather.15 = bf16[384,1152]{1,0:T(8,128)(2,1)S(1)} all-gather(bf16[192,1152]{1,0:T(8,128)(2,1)S(1)} %all_to_all.19), channel_id=1, replica_groups=mesh['rows'=16,'cols'=2] {'cols'}, dimensions={0}, use_global_device_ids=true | all-gather | bytes 1327104 | tf_op jit(solution)/shard_map/all_gather | solution.py:76
  32.3 0.1 add_reduce_fusion
  32.5 0.5 convolution_multiply_fusion.2
  33.0 0.8 broadcast_in_dim.19
  33.9 4.2 %all-to-all-start.1 = ((f32[16,64,128]{2,1,0:T(8,128)}), f32[16,64,128]{2,1,0:T(8,128)S(1)}, u32[]{:S(2)}, u32[]{:S(2)}) async-start(f32[16,64,128]{2,1,0:T(8,128)} %broadcast_in_dim.19), calls=%async_computation.1 | async-start | bytes 1048576 | tf_op jit(solution)/shard_map/all_to_all | solution.py:35
  38.1 6.5 %convolution_multiply_fusion = f32[64,4096]{1,0:T(8,128)S(1)} fusion(bf16[4096,1024]{1,0:T(8,128)(2,1)} %param.11, f32[4096]{0:T(1024)S(1)} %copy-done.1, bf16[384,1152]{1,0:T(8,128)(2,1)S(1)} %all_gather.15, f32[64]{0:T(128)S(1)} %copy-done.2, s32[384]{0:T(512)S(1)} %add_reduce_fusion), kind=kOutput, calls=%fused_computation.4 | convolution fusion | flops 3430703104 | bytes 10242560 | tf_op jit(solution)/shard_map/dot_general | solution.py:17
  44.6 1.8 %convolution_convert_fusion = bf16[128,4096]{1,0:T(8,128)(2,1)S(1)} fusion(f32[64,128]{1,0:T(8,128)S(1)} %convolution_multiply_fusion.2, f32[64,4096]{1,0:T(8,128)S(1)} %convolution_multiply_fusion), kind=kOutput, calls=%fused_computation.2 | convolution fusion | flops 403177472 | bytes 2129920 | tf_op jit(solution)/shard_map/dot_general | solution.py:17
  46.4 1.1 copy.51
  47.5 6.0 %all-to-all-done.1 = f32[16,64,128]{2,1,0:T(8,128)S(1)} async-done(((f32[16,64,128]{2,1,0:T(8,128)}), f32[16,64,128]{2,1,0:T(8,128)S(1)}, u32[]{:S(2)}, u32[]{:S(2)}) %all-to-all-start.1) | async-done | bytes 524320 | tf_op jit(solution)/shard_map/all_to_all | solution.py:35
  53.5 3.9 %all-to-all-start.2 = ((bf16[16,128,256]{2,1,0:T(8,128)(2,1)}), bf16[16,128,256]{2,1,0:T(8,128)(2,1)S(1)}, u32[]{:S(2)}, u32[]{:S(2)}) async-start(bf16[16,128,256]{2,1,0:T(8,128)(2,1)} %bitcast.67), calls=%async_computation.2 | async-start | bytes 2097152 | tf_op jit(solution)/shard_map/all_to_all | solution.py:94
  57.4 1.0 convolution_bitcast_fusion
  58.4 0.1 fusion.45
  58.6 0.6 select_reduce_fusion.3
  59.9 0.1 copy.36
  60.0 5.8 %cholesky.44 = f32[64,64]{1,0:T(8,128)S(1)} custom-call(f32[64,64]{1,0:T(8,128)S(1)} %fusion.36), custom_call_target="Cholesky" | custom-call | tf_op jit(solution)/shard_map/jit(cholesky)/cholesky | solution.py:43
  65.9 0.6 compare_reduce_fusion.1
  66.5 0.7 fusion.37
  67.2 4.9 %custom-call.6 = f32[1,64,64]{1,2,0:T(8,128)S(1)} custom-call(f32[1,64,64]{2,1,0:T(8,128)S(1)} %get-tuple-element.15), custom_call_target="InvertDiagBlocksLowerTriangular" | custom-call | tf_op jit(solution)/shard_map/jit(_solve_triangular)/triangular_solve | solution.py:44
  72.1 0.3 fusion.27
  72.3 0.2 fusion.31
  72.6 0.1 copy.48
  72.6 0.2 fusion.43
  72.8 0.2 convolution_subtract_fusion.4
  73.0 0.2 fusion.47
  73.3 0.8 select_reduce_fusion.2
  74.8 0.1 copy.41
  74.9 5.8 %cholesky.55 = f32[64,64]{1,0:T(8,128)S(1)} custom-call(f32[64,64]{1,0:T(8,128)S(1)} %fusion.34), custom_call_target="Cholesky" | custom-call | tf_op jit(solution)/shard_map/jit(cholesky)/cholesky | solution.py:43
  80.7 0.6 compare_reduce_fusion
  81.4 0.7 fusion.38
  82.1 4.9 %custom-call.7 = f32[1,64,64]{1,2,0:T(8,128)S(1)} custom-call(f32[1,64,64]{2,1,0:T(8,128)S(1)} %get-tuple-element.17), custom_call_target="InvertDiagBlocksLowerTriangular" | custom-call | tf_op jit(solution)/shard_map/jit(_solve_triangular)/triangular_solve | solution.py:44
  86.9 0.3 fusion.25
  87.2 0.1 convert_reduce_fusion
  87.4 0.2 fusion.46
  87.6 0.2 convolution_subtract_fusion.1
  87.8 0.2 convolution_convert_fusion.2
  88.0 0.1 copy.43
  88.1 1.2 broadcast_in_dim.21
  89.3 6.9 %all-to-all-start.3 = ((bf16[16,128,256]{1,2,0:T(8,128)(2,1)}), bf16[16,128,256]{1,2,0:T(8,128)(2,1)S(1)}, u32[]{:S(2)}, u32[]{:S(2)}) async-start(bf16[16,128,256]{1,2,0:T(8,128)(2,1)} %broadcast_in_dim.21), calls=%async_computation.3 | async-start | bytes 2097152 | tf_op jit(solution)/shard_map/all_to_all | solution.py:35
  96.2 0.1 copy.37
  96.3 0.2 fusion.29
  96.5 0.2 convolution_subtract_fusion.2
  96.7 0.2 fusion.48
  96.8 22.5 %all-to-all-done.3 = bf16[16,128,256]{1,2,0:T(8,128)(2,1)S(1)} async-done(((bf16[16,128,256]{1,2,0:T(8,128)(2,1)}), bf16[16,128,256]{1,2,0:T(8,128)(2,1)S(1)}, u32[]{:S(2)}, u32[]{:S(2)}) %all-to-all-start.3) | async-done | bytes 1048608 | tf_op jit(solution)/shard_map/all_to_all | solution.py:35
  119.3 1.2 convolution_subtract_fusion
  120.6 0.1 slice_select_fusion.1
  120.6 0.2 bitcast_convert_fusion
  120.8 0.1 slice.90
  121.0 0.5 copy-done
  121.5 0.1 slice_select_fusion
  121.6 0.1 maximum_multiply_fusion
  121.8 1.8 %copy.44 = f32[128,4096]{1,0:T(8,128)} copy(f32[128,4096]{0,1:T(8,128)S(1)} %maximum_multiply_fusion) | data formatting | bytes 4194304
  123.6 1.0 pad_maximum_fusion
  (21 shorter events, 0.2 us)
Async XLA Ops:
  0.6 15.4 %slice-start.1 = ((bf16[4096,1024]{1,0:T(8,128)(2,1)}), bf16[128,1024]{1,0:T(8,128)(2,1)S(1)}, s32[]{:S(2)}) async-start(bf16[4096,1024]{1,0:T(8,128)(2,1)} %param.11), calls=%async_computation.5 | async-start | bytes 524288 | tf_op jit(solution)/shard_map/slice | solution.py:56
  0.6 13.6 %copy-start.1 = (f32[4096]{0:T(1024)S(1)}, f32[4096]{0:T(1024)}, u32[]{:S(2)}) copy-start(f32[4096]{0:T(1024)} %param.12) | copy-start | bytes 49156
  4.3 28.2 %copy-start.2 = (f32[64]{0:T(128)S(1)}, f32[64]{0:T(128)}, u32[]{:S(2)}) copy-start(f32[64]{0:T(128)} %param.15) | copy-start | bytes 772
  5.2 24.6 %all-to-all-start = ((bf16[16,12,1152]{2,1,0:T(8,128)(2,1)}), bf16[16,12,1152]{2,1,0:T(8,128)(2,1)S(1)}, u32[]{:S(2)}, u32[]{:S(2)}) async-start(bf16[16,12,1152]{2,1,0:T(8,128)(2,1)} %all_to_all.17), calls=%async_computation | async-start | bytes 1179648 | tf_op jit(solution)/shard_map/all_to_all | solution.py:75
  33.9 19.6 %all-to-all-start.1 = ((f32[16,64,128]{2,1,0:T(8,128)}), f32[16,64,128]{2,1,0:T(8,128)S(1)}, u32[]{:S(2)}, u32[]{:S(2)}) async-start(f32[16,64,128]{2,1,0:T(8,128)} %broadcast_in_dim.19), calls=%async_computation.1 | async-start | bytes 1048576 | tf_op jit(solution)/shard_map/all_to_all | solution.py:35
  53.5 33.7 %all-to-all-start.2 = ((bf16[16,128,256]{2,1,0:T(8,128)(2,1)}), bf16[16,128,256]{2,1,0:T(8,128)(2,1)S(1)}, u32[]{:S(2)}, u32[]{:S(2)}) async-start(bf16[16,128,256]{2,1,0:T(8,128)(2,1)} %bitcast.67), calls=%async_computation.2 | async-start | bytes 2097152 | tf_op jit(solution)/shard_map/all_to_all | solution.py:94
  89.3 30.0 %all-to-all-start.3 = ((bf16[16,128,256]{1,2,0:T(8,128)(2,1)}), bf16[16,128,256]{1,2,0:T(8,128)(2,1)S(1)}, u32[]{:S(2)}, u32[]{:S(2)}) async-start(bf16[16,128,256]{1,2,0:T(8,128)(2,1)} %broadcast_in_dim.21), calls=%async_computation.3 | async-start | bytes 2097152 | tf_op jit(solution)/shard_map/all_to_all | solution.py:35
  120.5 1.0 copy-start
  121.8 1.8 %slice-start = ((f32[64,4096]{1,0:T(8,128)}), f32[64,3968]{1,0:T(8,128)S(1)}, s32[]{:S(2)}) async-start(f32[64,4096]{1,0:T(8,128)} %copy-done), calls=%async_computation.4 | async-start | bytes 2031616 | tf_op jit(solution)/shard_map/slice | solution.py:123
where the time goes:
time: 125 us
  waiting for transfers between devices  40 us (32%)
  other arithmetic  28.4 us (23%)
  starting transfers between devices  23.4 us (19%)
  matrix products  15.6 us (12%)
  local copies, waits for them, and re-layouts  7.86 us (6%)
  blocking collectives  6.42 us (5%)
  between operations  2.97 us (2%)
    all_to_all x2, waiting for transfers between devices, spread(): lax.all_to_all(jnp.broadcast_to(value[None], (size,) + value.shape), axis...  28.5 us
    dot_general x17, matrix products, mm(): lax.dot_general(left, right, ((contract[0], contract[1]), ((), ())), prec...  15.1 us
    another operation x6, other arithmetic, factor(): chol_lower = jnp.linalg.cholesky(gram_mat + shift * eye)  13 us
    all_to_all x1, waiting for transfers between devices, body(): arrived = lax.all_to_all(payload, 'rows', 0, 0, tiled=True)  11.6 us
    all_to_all x2, starting transfers between devices, spread(): lax.all_to_all(jnp.broadcast_to(value[None], (size,) + value.shape), axis...  11.1 us
    another operation x2, other arithmetic, factor(): jax.scipy.linalg.solve_triangular(chol_lower, eye, lower=True)  9.79 us
    all_to_all x1, starting transfers between devices, body(): arrived = lax.all_to_all(payload, 'rows', 0, 0, tiled=True)  8.34 us
    all_gather x2, blocking collectives, from_root(): return lax.all_gather(value, axis)[0]  3.98 us
  transfers between devices with their start and end apart: 4, of which 3 were waited for; matrix products, arithmetic and copies ran while one was open for 31% of the time, Pallas kernels for 0%

commit v1 on v0

v1 whole, which is shorter than its diff:
```python
import functools
import math

import jax
import jax.numpy as jnp
from jax import lax
from jax.experimental import pallas as pl
from jax.experimental.pallas import tpu as pltpu
from jax.sharding import PartitionSpec as P

PW = 64
PANELS = 2
WIDE = PW * PANELS
BLOCK = 128
LANES = 128
PIVOTS = 8
HI = lax.Precision.HIGHEST
F32 = jnp.float32
BF16 = jnp.bfloat16
MESH = pl.DeviceIdType.MESH


def mm(left, right, contract, precision=HI):
    return lax.dot_general(
        left, right, ((contract[0], contract[1]), ((), ())), precision=precision,
        preferred_element_type=F32,
    )


def eliminate(system):
    rows = lax.broadcasted_iota(jnp.int32, (PW, WIDE), 0)
    for k in range(0, PW, PIVOTS):
        rest, index = system[k:], rows[k:]
        cols = [
            jnp.broadcast_to(rest[:, k + j:k + j + 1], rest.shape) for j in range(PIVOTS)
        ]
        tops = [rest[j:j + 1] for j in range(PIVOTS)]
        for p in range(PIVOTS):
            mult = jnp.where(index > k + p, cols[p] * (1.0 / cols[p][p:p + 1]), 0.0)
            for j in range(p + 1, PIVOTS):
                cols[j] = cols[j] - mult * cols[j][p:p + 1]
                tops[j] = tops[j] - mult[j:j + 1] * tops[p]
            cols[p] = mult
        for p in range(PIVOTS):
            rest = rest - cols[p] * tops[p]
        system = jnp.concatenate([system[:k], rest], axis=0) if k else rest
    return system


def factor(gram, ridge):
    row = lax.broadcasted_iota(jnp.int32, (PW, PW), 0)
    col = lax.broadcasted_iota(jnp.int32, (PW, PW), 1)
    on = row == col
    trace = jnp.sum(jnp.sum(jnp.where(on, gram, 0.0), axis=1, keepdims=True), axis=0, keepdims=True)
    shift = ridge * trace / PW + 1e-06
    eye = on.astype(F32)
    system = eliminate(jnp.concatenate([gram + shift * eye, eye], axis=1))
    left = system[:, :PW]
    diag = jnp.sum(jnp.where(on, left, 0.0), axis=1, keepdims=True)
    scale = lax.rsqrt(diag)
    upper = jnp.where(col >= row, left * scale, 0.0)
    return upper, system[:, PW:] * scale, shift


def bit_of(index, bit):
    return (index // (1 << bit)) % 2


def split_bf16(value):
    high = value.astype(BF16)
    return high, (value - high.astype(F32)).astype(BF16)


def fit_kernel(
    owners, units, env_ref, label_ref, points_hbm, scale_ref, head_points_ref, head_scale_ref,
    weight_ref, ridge_ref,
    coupled_hbm, matrix_hbm, q_ref, r_head_ref,
    points, matrix, gram_out, gram_in, gram_sum, gram_all, acc, sent, got, whole,
    points_sem, out_sem, g_send, g_recv, h_send, h_recv, r_send, r_recv,
):
    me = lax.axis_index("rows")
    stages = owners.bit_length() - 1
    eq_count = weight_ref.shape[0]
    env_count, desc = env_ref.shape
    col_count = scale_ref.shape[1]
    unit_cols = col_count // units
    grow = WIDE // owners
    high = unit_cols // owners
    row_parts = WIDE // high

    loads = []
    for u in range(units):
        load = pltpu.make_async_copy(
            points_hbm.at[pl.ds(u * unit_cols, unit_cols)], points.at[u], points_sem.at[u]
        )
        load.start()
        loads.append(load)

    barrier = pltpu.get_barrier_semaphore()

    def greet(d, _):
        pl.semaphore_signal(
            barrier, inc=1, device_id={"rows": (me + d) % owners}, device_id_type=MESH
        )
        return 0

    lax.fori_loop(1, owners, greet, 0)

    env_rows = env_ref[...]
    targets = lax.broadcasted_iota(jnp.int32, (eq_count, env_count), 0)
    selector = jnp.where(label_ref[...] == targets, 1.0, 0.0).astype(BF16)
    weight = weight_ref[...]

    def equations(rows, scale):
        products = mm(env_rows, rows, ((1,), (1,)), None) * desc ** (-0.5)
        squared = products * products
        kernel = (scale * squared * squared).astype(BF16)
        return mm(selector, kernel, ((1,), (0,)), None) * weight

    head = equations(head_points_ref[...], head_scale_ref[...])
    gram = mm(head, head, ((0,), (0,)))
    for p in range(owners):
        gram_out[p] = gram[p * grow:(p + 1) * grow]
    pl.semaphore_wait(barrier, owners - 1)

    def spread(src_of, slots, send, recv):
        def start(d, _):
            to = (me + d) % owners
            pltpu.make_async_remote_copy(
                src_ref=src_of(to), dst_ref=slots.at[me], send_sem=send.at[to],
                recv_sem=recv.at[me], device_id={"rows": to}, device_id_type=MESH,
            ).start()
            return 0

        lax.fori_loop(1, owners, start, 0)

    def collect(src_of, slots, send, recv):
        def end(d, _):
            other = (me + d) % owners
            copy = pltpu.make_async_remote_copy(
                src_ref=src_of(other), dst_ref=slots.at[other], send_sem=send.at[other],
                recv_sem=recv.at[other], device_id={"rows": other}, device_id_type=MESH,
            )
            copy.wait_send()
            copy.wait_recv()
            return 0

        lax.fori_loop(1, owners, end, 0)

    spread(lambda to: gram_out.at[to], gram_in, g_send, g_recv)
    gram_in[me] = gram_out[me]

    def unit_matrix(u):
        loads[u].wait()
        cols = slice(u * unit_cols, (u + 1) * unit_cols)
        matrix[u] = equations(points[u], scale_ref[:, cols])
        out = pltpu.make_async_copy(matrix.at[u], matrix_hbm.at[u], out_sem.at[0, u])
        out.start()
        return out

    outs = []
    for u in range(units // 2):
        outs.append(unit_matrix(u))
    collect(lambda to: gram_out.at[to], gram_in, g_send, g_recv)
    total = gram_in[0]
    for p in range(1, owners):
        total = total + gram_in[p]
    gram_sum[...] = total
    spread(lambda to: gram_sum, gram_all, h_send, h_recv)
    gram_all[me] = total
    for u in range(units // 2, units):
        outs.append(unit_matrix(u))
    collect(lambda to: gram_sum, gram_all, h_send, h_recv)
    gram = jnp.concatenate([gram_all[p] for p in range(owners)], axis=0)

    ridge = ridge_ref[...]
    up1, inv1, shift = factor(gram[:PW, :PW], ridge)
    c12 = mm(inv1, gram[:PW, PW:], ((1,), (0,)))
    back = mm(inv1, c12, ((0,), (0,)))
    pair = jnp.concatenate([c12, jnp.sqrt(shift) * back], axis=0)
    up2, inv2, _ = factor(gram[PW:, PW:] - mm(pair, pair, ((0,), (0,))), ridge)
    q1 = mm(head[:, :PW], inv1, ((1,), (1,)))
    q2 = mm(head[:, PW:] - mm(q1, c12, ((1,), (0,))), inv2, ((1,), (1,)))
    deep = c12 + shift * mm(inv1, back, ((1,), (0,)))
    w2 = mm(head[:, PW:] - mm(q1, deep, ((1,), (0,))), inv2, ((1,), (1,)))
    q_ref[...] = jnp.concatenate([q1, q2], axis=1)
    r_head_ref[...] = jnp.concatenate(
        [
            jnp.concatenate([up1, c12], axis=1),
            jnp.concatenate([jnp.zeros((PW, PW), F32), up2], axis=1),
        ],
        axis=0,
    )
    w_high, w_low = split_bf16(jnp.concatenate([q1, w2], axis=1).T)
    w_wide = jnp.concatenate([w_high, w_low, w_high], axis=1)

    def order(u):
        bits = list(range(stages))
        if u % 2 and stages > 1:
            bits[0], bits[1] = 1, 0
        return bits

    def start_of(u, t):
        bits = order(u)
        return sum(
            (bit_of(me, bits[i]) * (owners >> (i + 1)) for i in range(t)), jnp.int32(0)
        )

    def reduce_copy(u, t):
        mine = bit_of(me, order(u)[t])
        half = owners >> (t + 1)
        step = 1 << order(u)[t]
        first = start_of(u, t) + (1 - mine) * half
        return pltpu.make_async_remote_copy(
            src_ref=sent.at[u, pl.ds(first, half)],
            dst_ref=got.at[u, pl.ds(owners - 2 * half, half)],
            send_sem=r_send.at[u, t], recv_sem=r_recv.at[u, t],
            device_id={"rows": me + (1 - 2 * mine) * step}, device_id_type=MESH,
        )

    def gather_copy(u, t):
        mine = bit_of(me, order(u)[t])
        half = owners >> (t + 1)
        step = 1 << order(u)[t]
        first = start_of(u, t + 1)
        return pltpu.make_async_remote_copy(
            src_ref=whole.at[u, pl.ds(first, half)],
            dst_ref=whole.at[u, pl.ds(first, half)],
            send_sem=r_send.at[u, stages + t], recv_sem=r_recv.at[u, stages + t],
            device_id={"rows": me + (1 - 2 * mine) * step}, device_id_type=MESH,
        )

    def open_unit(u):
        m_high, m_low = split_bf16(matrix[u])
        part = mm(
            w_wide, jnp.concatenate([m_high, m_high, m_low], axis=0), ((1,), (0,)), None
        )
        for p in range(owners):
            row, col = (p % row_parts) * high, (p // row_parts) * LANES
            piece = part[row:row + high, col:col + LANES]
            acc[u, p] = piece
            sent[u, p] = piece.astype(BF16)
        reduce_copy(u, 0).start()

    def reduce_step(u, t):
        copy = reduce_copy(u, t)
        copy.wait_recv()
        half = owners >> (t + 1)
        keep = start_of(u, t + 1)
        value = acc[u, pl.ds(keep, half)] + got[
            u, pl.ds(owners - 2 * half, half)
        ].astype(F32)
        if t + 1 < stages:
            acc[u, pl.ds(keep, half)] = value
            sent[u, pl.ds(keep, half)] = value.astype(BF16)
            reduce_copy(u, t + 1).start()
        else:
            whole[u, pl.ds(keep, half)] = value.astype(BF16)
            gather_copy(u, t).start()

    def gather_step(u, t):
        gather_copy(u, t).wait_recv()
        if t:
            gather_copy(u, t - 1).start()
        else:
            out = pltpu.make_async_copy(whole.at[u], coupled_hbm.at[u], out_sem.at[1, u])
            out.start()
            outs.append(out)

    def run(u, s):
        if s == 0:
            open_unit(u)
        elif s <= stages:
            reduce_step(u, s - 1)
        else:
            gather_step(u, 2 * stages - s)

    lag = 2
    steps = 2 * stages + 1
    for wave in range(steps + lag * ((units - 1) // 2)):
        for u in range(units):
            s = wave - lag * (u // 2)
            if 0 <= s < steps:
                run(u, s)
    for u in range(units):
        for t in range(stages):
            reduce_copy(u, t).wait_send()
            gather_copy(u, t).wait_send()
    for out in outs:
        out.wait()


def fit(env_rows, labels, points, scale, head_points, head_scale, row_weight, ridge, owners, units):
    col_count, desc = points.shape
    unit_cols = col_count // units
    eq_count = row_weight.shape[0]
    high = unit_cols // owners
    stages = owners.bit_length() - 1
    grow = WIDE // owners
    vmem = pl.BlockSpec(memory_space=pltpu.VMEM)
    hbm = pl.BlockSpec(memory_space=pl.ANY)
    dma = pltpu.SemaphoreType.DMA
    return pl.pallas_call(
        functools.partial(fit_kernel, owners, units),
        out_shape=(
            jax.ShapeDtypeStruct((units, owners, high, LANES), BF16),
            jax.ShapeDtypeStruct((units, eq_count, unit_cols), F32),
            jax.ShapeDtypeStruct((eq_count, WIDE), F32),
            jax.ShapeDtypeStruct((WIDE, WIDE), F32),
        ),
        in_specs=[vmem, vmem, hbm, vmem, vmem, vmem, vmem, vmem],
        out_specs=(hbm, hbm, vmem, vmem),
        scratch_shapes=[
            pltpu.VMEM((units, unit_cols, desc), BF16),
            pltpu.VMEM((units, eq_count, unit_cols), F32),
            pltpu.VMEM((owners, grow, WIDE), F32),
            pltpu.VMEM((owners, grow, WIDE), F32),
            pltpu.VMEM((grow, WIDE), F32),
            pltpu.VMEM((owners, grow, WIDE), F32),
            pltpu.VMEM((units, owners, high, LANES), F32),
            pltpu.VMEM((units, owners, high, LANES), BF16),
            pltpu.VMEM((units, owners, high, LANES), BF16),
            pltpu.VMEM((units, owners, high, LANES), BF16),
            dma((units,)),
            dma((2, units)),
            dma((owners,)),
            dma((owners,)),
            dma((owners,)),
            dma((owners,)),
            dma((units, 2 * stages)),
            dma((units, 2 * stages)),
        ],
        compiler_params=pltpu.CompilerParams(collective_id=0, has_side_effects=True),
    )(
        env_rows, labels.reshape(1, -1), points, scale.reshape(1, -1), head_points,
        head_scale.reshape(1, -1), row_weight.reshape(-1, 1), ridge.reshape(1, 1),
    )


def finish_kernel(norm_scale, coupled_ref, matrix_ref, q_ref, r_head_ref, r_ref, reduced_ref):
    owners, high, _ = coupled_ref.shape[1:]
    row_parts = WIDE // high
    cols = [
        jnp.concatenate([coupled_ref[0, c * row_parts + r] for r in range(row_parts)], axis=0)
        for c in range(owners // row_parts)
    ]
    coupled = jnp.concatenate(cols, axis=1)
    q_cols = q_ref[...]
    q_high, q_low = split_bf16(q_cols)
    update = mm(
        jnp.concatenate([q_high, q_low], axis=1), jnp.concatenate([coupled, coupled], axis=0),
        ((1,), (0,)), None,
    )
    r_ref[...] = coupled.astype(F32) * norm_scale
    reduced_ref[...] = matrix_ref[0] - update

    @pl.when((lax.axis_index("cols") == 0) & (pl.program_id(0) == 0))
    def _():
        r_ref[:, :WIDE] = r_head_ref[...] * norm_scale
        reduced_ref[:, :WIDE] = q_cols


def finish(coupled, matrix, q_cols, r_head, norm_scale):
    units, owners, high, _ = coupled.shape
    _, eq_count, unit_cols = matrix.shape
    return pl.pallas_call(
        functools.partial(finish_kernel, norm_scale),
        grid=(units,),
        out_shape=(
            jax.ShapeDtypeStruct((WIDE, units * unit_cols), F32),
            jax.ShapeDtypeStruct((eq_count, units * unit_cols), F32),
        ),
        in_specs=[
            pl.BlockSpec((1, owners, high, LANES), lambda u: (u, 0, 0, 0)),
            pl.BlockSpec((1, eq_count, unit_cols), lambda u: (u, 0, 0)),
            pl.BlockSpec((eq_count, WIDE), lambda u: (0, 0)),
            pl.BlockSpec((WIDE, WIDE), lambda u: (0, 0)),
        ],
        out_specs=(
            pl.BlockSpec((WIDE, unit_cols), lambda u: (0, u)),
            pl.BlockSpec((eq_count, unit_cols), lambda u: (0, u)),
        ),
    )(coupled, matrix, q_cols, r_head)


def from_root(value, axis):
    return lax.all_gather(value, axis)[0]


def body(
    descriptors, sparse_points, point_scale, env_owner, env_structure, row_weight, ridge_factor
):
    owners = lax.axis_size("rows")
    col_index = lax.axis_index("cols")
    eq_count = row_weight.shape[0]
    env_local, desc = descriptors.shape
    col_count = sparse_points.shape[0]

    head_points = from_root(sparse_points[:WIDE], "cols")
    head_scale = from_root(point_scale[:WIDE], "cols")

    per_block = max(2, (3 * BLOCK + 2 * owners - 1) // (2 * owners))
    capacity = min(env_local, per_block * (-(-env_local // BLOCK)))
    own = lax.dynamic_slice_in_dim(env_owner[:, 0], col_index * env_local, env_local)
    struct = lax.dynamic_slice_in_dim(env_structure, col_index * env_local, env_local)
    idx = jnp.arange(env_local)
    within = jnp.sum(
        ((own[:, None] == own[None, :]) & (idx[None, :] < idx[:, None])).astype(jnp.int32), axis=1
    )
    slot = own * capacity + within
    slots = lax.broadcasted_iota(jnp.int32, (owners * capacity, env_local), 0)
    pick = (slots == slot[None, :]).astype(BF16)
    lane = lax.broadcasted_iota(jnp.int32, (env_local, LANES), 1)
    tag = jnp.where(lane == 0, struct[:, None] + 1, 0).astype(BF16)
    payload = mm(
        pick, jnp.concatenate([descriptors, tag], axis=1), ((1,), (0,)), None
    ).astype(BF16)
    arrived = lax.all_to_all(payload, "rows", 0, 0, tiled=True)
    arrived = lax.all_gather(arrived, "cols", axis=0, tiled=True)
    env_rows = arrived[:, :desc]
    labels = arrived[:, desc].astype(jnp.int32) - 1

    units = max(1, min(8, col_count // (16 * owners)))
    coupled, matrix, q_cols, r_head = fit(
        env_rows, labels, sparse_points, point_scale, head_points, head_scale, row_weight,
        ridge_factor, owners, units,
    )
    return finish(coupled, matrix, q_cols, r_head, 1.0 / math.sqrt(owners * eq_count))


def solution(mesh):
    return jax.shard_map(
        body,
        mesh=mesh,
        in_specs=(
            P(("rows", "cols"), None),
            P("cols", None),
            P("cols"),
            P("rows", None),
            P("rows"),
            P("rows"),
            P(),
        ),
        out_specs=(P(None, "cols"), P("rows", "cols")),
        check_vma=False,
    )
```

time: 125 us -> 109 us (0.87)
  Pallas kernels: 0 us -> 74.2 us
  waiting for transfers between devices: 40 us -> 7.29 us
  other arithmetic: 28.4 us -> 1.83 us
  starting transfers between devices: 23.4 us -> 8.34 us
  matrix products: 15.6 us -> 1.22 us
  between operations: 2.97 us -> 1.34 us
    pallas_call x0 -> x2, Pallas kernels: none -> 74.2 us  [the longest x1 67.6 us: fit(): pl.pallas_call(functools.partial(fit_kernel, owners, units), out_shape=(j...]
    all_to_all x3 -> x0, waiting for transfers between devices: 28.5 us -> none  [the longest x2 28.5 us: spread(): lax.all_to_all(jnp.broadcast_to(value[None], (size,) + value.shape), axis...]
    another operation x8 -> x0, other arithmetic: 22.8 us -> none  [the longest x6 13 us: factor(): chol_lower = jnp.linalg.cholesky(gram_mat + shift * eye)]
    all_to_all x3 -> x0, starting transfers between devices: 15.1 us -> none  [the longest x2 11.1 us: spread(): lax.all_to_all(jnp.broadcast_to(value[None], (size,) + value.shape), axis...]
    dot_general x17 -> x1, matrix products: 15.1 us -> 1.22 us  [mm(): lax.dot_general(left, right, ((contract[0], contract[1]), ((), ())), prec...]
    all_to_all x1, waiting for transfers between devices: 11.6 us -> 7.29 us  [body(): arrived = lax.all_to_all(payload, 'rows', 0, 0, tiled=True)]
    broadcast_in_dim x2 -> x0, local copies, waits for them, and re-layouts: 2.02 us -> none  [spread(): jnp.broadcast_to(value[None], (size,) + value.shape)]
    unnamed x11 -> x1, local copies, waits for them, and re-layouts: 2.6 us -> 0.69 us
  transfers between devices with their start and end apart: 4 -> 1, of which waited for: 3 -> 1; matrix products, arithmetic and copies ran while one was open for 31% -> 4% of each run, Pallas kernels for 0% -> 0%
where the time goes in v1:
time: 109 us; the launch traced here: 108 us
  Pallas kernels  74.2 us (68%)
  starting transfers between devices  8.34 us (8%)
  local copies, waits for them, and re-layouts  7.55 us (7%)
  waiting for transfers between devices  7.29 us (7%)
  blocking collectives  6.42 us (6%)
  other arithmetic  1.83 us (2%)
  between operations  1.34 us (1%)
  matrix products  1.22 us (1%)
    pallas_call x1, Pallas kernels, fit(): pl.pallas_call(functools.partial(fit_kernel, owners, units), out_shape=(j...  67.6 us
    all_to_all x1, starting transfers between devices, body(): arrived = lax.all_to_all(payload, 'rows', 0, 0, tiled=True)  8.34 us
    all_to_all x1, waiting for transfers between devices, body(): arrived = lax.all_to_all(payload, 'rows', 0, 0, tiled=True)  7.29 us
    pallas_call x1, Pallas kernels, finish(): pl.pallas_call(functools.partial(finish_kernel, norm_scale), grid=(units,...  6.6 us
    all_gather x2, blocking collectives, from_root(): return lax.all_gather(value, axis)[0]  3.98 us
    all_gather x1, blocking collectives, body(): arrived = lax.all_gather(arrived, 'cols', axis=0, tiled=True)  2.44 us
  transfers between devices with their start and end apart: 1, of which 1 were waited for; matrix products, arithmetic and copies ran while one was open for 4% of the time, Pallas kernels for 0%

profile of v1, /device:TPU:0, one launch (start us, length us, event | category | flops | bytes accessed | tf_op | source)
XLA Modules:
  0.0 108.2 jit_solution(8095345556968756905)
XLA Ops:
  0.6 0.8 dynamic-slice_add_fusion
  1.4 0.7 dynamic-slice_bitcast_fusion
  2.1 0.2 convert_reduce_fusion
  2.2 0.7 multiply_add_fusion
  2.9 0.1 select_convert_fusion
  3.0 1.2 %convolution_convert_fusion = bf16[192,1152]{1,0:T(8,128)(2,1)S(1)} fusion(bf16[128,128]{1,0:T(8,128)(2,1)S(1)} %select_convert_fusion, bf16[128,1024]{1,0:T(8,128)(2,1)} %param.7, s32[128]{0:T(128)S(1)} %multiply_add_fusion), kind=kOutput, calls=%fused_computation | convolution fusion | flops 57458688 | bytes 737792 | tf_op jit(solution)/shard_map/dot_general | solution.py:24
  4.2 0.9 all_to_all.8
  5.1 8.3 %all-to-all-start = ((bf16[16,12,1152]{2,1,0:T(8,128)(2,1)}), bf16[16,12,1152]{2,1,0:T(8,128)(2,1)S(1)}, u32[]{:S(2)}, u32[]{:S(2)}) async-start(bf16[16,12,1152]{2,1,0:T(8,128)(2,1)} %all_to_all.8), calls=%async_computation | async-start | bytes 1179648 | tf_op jit(solution)/shard_map/all_to_all | solution.py:418
  14.1 1.3 %copy.12.weight_ref = f32[64,1]{1,0:T(8,128)} copy(f32[64,1]{0,1:T(1,128)} %bitcast.13) | data formatting | bytes 512 | tf_op jit(solution)/shard_map/reshape | solution.py:336
  15.5 1.0 slice.20
  16.4 2.2 %all-gather = bf16[256,1024]{1,0:T(8,128)(2,1)S(1)} all-gather(bf16[128,1024]{1,0:T(8,128)(2,1)S(1)} %slice.20), channel_id=2, replica_groups=mesh['rows'=16,'cols'=2] {'cols'}, dimensions={0}, use_global_device_ids=true | all-gather | bytes 786432 | tf_op jit(solution)/shard_map/all_gather | solution.py:387
  18.6 0.7 slice.29.head_points_ref
  19.4 0.7 slice_bitcast_fusion.1
  20.0 1.8 %all-gather.2 = f32[2,1,128]{2,1,0:T(1,128)S(1)} all-gather(f32[1,1,128]{2,1,0:T(1,128)S(1)} %slice_bitcast_fusion.1), channel_id=3, replica_groups=mesh['rows'=16,'cols'=2] {'cols'}, dimensions={0}, use_global_device_ids=true | all-gather | bytes 1536 | tf_op jit(solution)/shard_map/all_gather | solution.py:387
  21.8 0.6 slice_bitcast_fusion.head_scale_ref
  22.4 7.3 %all-to-all-done = bf16[16,12,1152]{2,1,0:T(8,128)(2,1)S(1)} async-done(((bf16[16,12,1152]{2,1,0:T(8,128)(2,1)}), bf16[16,12,1152]{2,1,0:T(8,128)(2,1)S(1)}, u32[]{:S(2)}, u32[]{:S(2)}) %all-to-all-start) | async-done | bytes 442400 | tf_op jit(solution)/shard_map/all_to_all | solution.py:418
  29.7 0.1 all_to_all.10
  29.8 2.4 %all_gather.15 = bf16[384,1152]{1,0:T(8,128)(2,1)S(1)} all-gather(bf16[192,1152]{1,0:T(8,128)(2,1)S(1)} %all_to_all.10), channel_id=1, replica_groups=mesh['rows'=16,'cols'=2] {'cols'}, dimensions={0}, use_global_device_ids=true | all-gather | bytes 1327104 | tf_op jit(solution)/shard_map/all_gather | solution.py:419
  32.2 0.1 add_reduce_fusion
  32.4 1.0 slice.27.env_ref
  33.4 0.6 sub.7.label_ref
  34.0 67.6 %shard_map.86 = (bf16[8,16,32,128]{3,2,1,0:T(8,128)(2,1)}, f32[8,64,512]{2,1,0:T(8,128)}, f32[64,128]{1,0:T(8,128)}, f32[128,128]{1,0:T(8,128)}) custom-call(bf16[384,1024]{1,0:T(8,128)(2,1)} %slice.27.env_ref, s32[1,384]{1,0:T(1,128)} %sub.7.label_ref, bf16[4096,1024]{1,0:T(8,128)(2,1)} %points_hbm.1, f32[1,4096]{1,0:T(1,128)} %bitcast.12, ...), custom_call_target="tpu_custom_call" | custom-call | tf_op jit(solution)/shard_map/pallas_call | solution.py:303
  101.6 6.6 %shard_map.87 = (f32[128,4096]{1,0:T(8,128)}, f32[64,4096]{1,0:T(8,128)}) custom-call(bf16[8,16,32,128]{3,2,1,0:T(8,128)(2,1)} %get-tuple-element.6.coupled_ref, f32[8,64,512]{2,1,0:T(8,128)} %get-tuple-element.7.matrix_ref, f32[64,128]{1,0:T(8,128)} %get-tuple-element.8.q_ref, f32[128,128]{1,0:T(8,128)} %get-tuple-element.9.r_head_ref), custom_call_target="tpu_custom_call" | custom-call | tf_op jit(solution)/shard_map/pallas_call | solution.py:366
  (1 shorter events, 0.0 us)
Async XLA Ops:
  5.1 24.6 %all-to-all-start = ((bf16[16,12,1152]{2,1,0:T(8,128)(2,1)}), bf16[16,12,1152]{2,1,0:T(8,128)(2,1)S(1)}, u32[]{:S(2)}, u32[]{:S(2)}) async-start(bf16[16,12,1152]{2,1,0:T(8,128)(2,1)} %all_to_all.8), calls=%async_computation | async-start | bytes 1179648 | tf_op jit(solution)/shard_map/all_to_all | solution.py:418

commit v2 on v1

v2 whole, which is shorter than its diff:
```python
import functools
import math

import jax
import jax.numpy as jnp
from jax import lax
from jax.experimental import pallas as pl
from jax.experimental.pallas import tpu as pltpu
from jax.sharding import PartitionSpec as P

PW = 64
PANELS = 2
WIDE = PW * PANELS
BLOCK = 128
LANES = 128
PIVOTS = 8
UNITS = 4
LAG = 0.3
HI = lax.Precision.HIGHEST
F32 = jnp.float32
BF16 = jnp.bfloat16
MESH = pl.DeviceIdType.MESH


def mm(left, right, contract, precision=HI):
    return lax.dot_general(
        left, right, ((contract[0], contract[1]), ((), ())), precision=precision,
        preferred_element_type=F32,
    )


def eliminate(system):
    rows = lax.broadcasted_iota(jnp.int32, (PW, WIDE), 0)
    for k in range(0, PW, PIVOTS):
        rest, index = system[k:], rows[k:]
        cols = [
            jnp.broadcast_to(rest[:, k + j:k + j + 1], rest.shape) for j in range(PIVOTS)
        ]
        tops = [rest[j:j + 1] for j in range(PIVOTS)]
        for p in range(PIVOTS):
            mult = jnp.where(index > k + p, cols[p] * (1.0 / cols[p][p:p + 1]), 0.0)
            for j in range(p + 1, PIVOTS):
                cols[j] = cols[j] - mult * cols[j][p:p + 1]
                tops[j] = tops[j] - mult[j:j + 1] * tops[p]
            cols[p] = mult
        for p in range(PIVOTS):
            rest = rest - cols[p] * tops[p]
        system = jnp.concatenate([system[:k], rest], axis=0) if k else rest
    return system


def factor(gram, ridge):
    row = lax.broadcasted_iota(jnp.int32, (PW, PW), 0)
    col = lax.broadcasted_iota(jnp.int32, (PW, PW), 1)
    on = row == col
    trace = jnp.sum(jnp.sum(jnp.where(on, gram, 0.0), axis=1, keepdims=True), axis=0, keepdims=True)
    shift = ridge * trace / PW + 1e-06
    eye = on.astype(F32)
    system = eliminate(jnp.concatenate([gram + shift * eye, eye], axis=1))
    left = system[:, :PW]
    diag = jnp.sum(jnp.where(on, left, 0.0), axis=1, keepdims=True)
    scale = lax.rsqrt(diag)
    upper = jnp.where(col >= row, left * scale, 0.0)
    return upper, system[:, PW:] * scale, shift


def bit_of(index, bit):
    return (index // (1 << bit)) % 2


def split_bf16(value):
    high = value.astype(BF16)
    return high, (value - high.astype(F32)).astype(BF16)


def fit_kernel(
    owners, cores, units, groups, tail,
    desc_ref, owner_ref, struct_ref, points_hbm, scale_ref, weight_ref, ridge_ref,
    coupled_hbm, matrix_hbm, q_ref, r_head_ref,
    points, head_points, head_scale, keys, parcel, landed, env, matrix,
    gram_out, gram_in, gram_sum, gram_all, acc, sent, got, spot, whole,
    points_sem, out_sem, root_sem, root_send, root_recv, e_send, e_recv, f_send, f_recv,
    g_send, g_recv, h_send, h_recv, r_send, r_recv,
):
    me = lax.axis_index("rows")
    core = lax.axis_index("cols")
    env_local, desc = desc_ref.shape
    eq_count = weight_ref.shape[1]
    col_count = scale_ref.shape[1]
    unit_cols = col_count // units
    grow = WIDE // owners
    high = unit_cols // owners
    row_parts = WIDE // high
    line = owners // 4
    half_desc = desc // 2

    barrier = pltpu.get_barrier_semaphore()

    def greet_rows(d, _):
        pl.semaphore_signal(
            barrier, inc=1, device_id={"rows": (me + d) % owners}, device_id_type=MESH
        )
        return 0

    def greet_cols(d, _):
        pl.semaphore_signal(
            barrier, inc=1, device_id={"cols": (core + d) % cores}, device_id_type=MESH
        )
        return 0

    lax.fori_loop(1, owners, greet_rows, 0)
    lax.fori_loop(1, cores, greet_cols, 0)

    loads = []
    for u in range(units):
        load = pltpu.make_async_copy(
            points_hbm.at[pl.ds(u * unit_cols, unit_cols)], points.at[u], points_sem.at[u]
        )
        load.start()
        loads.append(load)

    def as_column(row):
        return jnp.broadcast_to(row.astype(F32), (LANES, row.shape[1])).T

    keys[0] = as_column(owner_ref[...])
    keys[1] = as_column(struct_ref[...])
    mine = pl.ds(pl.multiple_of(core * env_local, 8), env_local)
    own, struct = keys[0, mine], keys[1, mine]
    lane = lax.broadcasted_iota(jnp.int32, (env_local, LANES), 1).astype(F32)
    named = own == lane
    before = (
        lax.broadcasted_iota(jnp.int32, (env_local, env_local), 0)
        > lax.broadcasted_iota(jnp.int32, (env_local, env_local), 1)
    )
    ahead = mm(
        jnp.where(before, 1.0, 0.0).astype(BF16), jnp.where(named, 1.0, 0.0).astype(BF16),
        ((1,), (0,)), None,
    )
    within = jnp.sum(jnp.where(named, ahead, 0.0), axis=1, keepdims=True)
    own, struct = own[:, :1], struct[:, :1]
    place = lax.broadcasted_iota(jnp.int32, (env_local, owners * 8), 1).astype(F32)

    def pick(first, count, shift):
        inside = (within >= first) & (within < first + count)
        spot_of = jnp.where(inside, own * 8 + (within - first) + shift, -1.0)
        return jnp.where(place == spot_of, 1.0, 0.0).astype(BF16)

    descriptors = desc_ref[...]
    label = jnp.zeros((owners * 8, LANES), F32)
    for g in range(groups):
        chosen = pick(8 * g, 8, 0)
        block = mm(chosen, descriptors, ((0,), (0,)), None)
        parcel[:, :, g * desc:(g + 1) * desc] = block.reshape(owners, 8, desc).astype(BF16)
        tag = jnp.where(lane == g, struct + 1.0, 0.0).astype(BF16)
        label = label + mm(chosen, tag, ((0,), (0,)), None)
    edge = groups * desc
    if tail:
        lower, upper = pick(8 * groups, 4, 0), pick(8 * groups, 4, 4)
        block = mm(lower, descriptors[:, :half_desc], ((0,), (0,)), None) + mm(
            upper, descriptors[:, half_desc:], ((0,), (0,)), None
        )
        parcel[:, :, edge:edge + half_desc] = block.reshape(owners, 8, half_desc).astype(BF16)
        tag = jnp.where(lane == groups, struct + 1.0, 0.0).astype(BF16)
        label = label + mm(lower, tag, ((0,), (0,)), None)
        edge = edge + half_desc
    parcel[:, :, edge:] = label.reshape(owners, 8, LANES).astype(BF16)

    pl.semaphore_wait(barrier, owners + cores - 2)

    def exchange(src_of, slot_of, send, recv):
        def copy(to, sender):
            return pltpu.make_async_remote_copy(
                src_ref=src_of(to), dst_ref=slot_of(sender), send_sem=send.at[to],
                recv_sem=recv.at[sender], device_id={"rows": to}, device_id_type=MESH,
            )

        def start(d, _):
            copy((me + d) % owners, me).start()
            return 0

        def end(d, _):
            other = (me + d) % owners
            copy(other, other).wait_send()
            copy(other, other).wait_recv()
            return 0

        return start, end, copy

    start, _, routed = exchange(
        lambda to: parcel.at[to], lambda sender: landed.at[core, sender], e_send, e_recv
    )
    lax.fori_loop(1, owners, start, 0)

    def root_copies(to):
        pair = []
        for i, (src, dst) in enumerate(
            ((points_hbm.at[pl.ds(0, WIDE)], head_points), (scale_ref.at[:, pl.ds(0, WIDE)], head_scale))
        ):
            pair.append(
                pltpu.make_async_remote_copy(
                    src_ref=src, dst_ref=dst, send_sem=root_send.at[i, to],
                    recv_sem=root_recv.at[i], device_id={"cols": to}, device_id_type=MESH,
                )
            )
        return pair

    own_points = pltpu.make_async_copy(points_hbm.at[pl.ds(0, WIDE)], head_points, root_sem)

    @pl.when(core == 0)
    def _():
        own_points.start()
        head_scale[...] = scale_ref[:, :WIDE]
        for to in range(1, cores):
            for copy in root_copies(to):
                copy.start()

    def pass_on(slot, to, sender):
        return pltpu.make_async_remote_copy(
            src_ref=landed.at[sender, slot], dst_ref=landed.at[sender, slot],
            send_sem=f_send.at[to, slot], recv_sem=f_recv.at[sender, slot],
            device_id={"cols": to}, device_id_type=MESH,
        )

    def pass_all(slot):
        def one(d, _):
            pass_on(slot, (core + d) % cores, core).start()
            return 0

        lax.fori_loop(1, cores, one, 0)

    landed[core, me] = parcel[me]
    pass_all(me)

    def land(d, _):
        other = (me + d) % owners
        routed(other, other).wait_recv()
        pass_all(other)
        return 0

    lax.fori_loop(1, owners, land, 0)

    @pl.when(core == 0)
    def _():
        own_points.wait()
        for to in range(1, cores):
            for copy in root_copies(to):
                copy.wait_send()

    @pl.when(core != 0)
    def _():
        for copy in root_copies(0):
            copy.wait_recv()

    def passed(i, _):
        slot = i % owners
        other = (core + 1 + i // owners) % cores
        pass_on(slot, other, other).wait_recv()
        return 0

    lax.fori_loop(0, owners * (cores - 1), passed, 0)

    targets = lax.broadcasted_iota(jnp.int32, (1, LANES), 1).astype(F32)
    low_half = lax.broadcasted_iota(jnp.int32, (owners // 2, 8, 1), 1) < 4
    marks = []
    row = 0

    def swap(value):
        return jnp.concatenate([value[:, 4:], value[:, :4]], axis=1)

    def evens(value):
        paired = value.reshape((owners // 2, 2) + value.shape[1:])
        return paired[:, 0], paired[:, 1]

    for c in range(cores):
        tags = landed[c, :, :, edge:].astype(F32)
        for g in range(groups):
            env[row:row + owners * 8] = landed[c, :, :, g * desc:(g + 1) * desc].astype(
                F32
            ).reshape(owners * 8, desc).astype(BF16)
            tag = tags[:, :, g:g + 1].reshape(owners * 8, 1) - 1.0
            marks.append(jnp.where(tag == targets, 1.0, 0.0))
            row += owners * 8
        if tail:
            first, second = evens(
                landed[c, :, :, groups * desc:groups * desc + half_desc].astype(F32)
            )
            left = jnp.where(low_half, first, swap(second))
            right = jnp.where(low_half, swap(first), second)
            env[row:row + owners * 4, :half_desc] = left.reshape(owners * 4, half_desc).astype(BF16)
            env[row:row + owners * 4, half_desc:] = right.reshape(owners * 4, half_desc).astype(BF16)
            first, second = evens(jnp.broadcast_to(tags[:, :, groups:groups + 1], tags.shape))
            tag = jnp.where(low_half, first, swap(second)).reshape(owners * 4, LANES) - 1.0
            marks.append(jnp.where(tag == targets, 1.0, 0.0))
            row += owners * 4
    selector = jnp.concatenate(marks, axis=0).T[:eq_count].astype(BF16)
    weight = as_column(weight_ref[...])[:, :1]

    def equations(rows, scale):
        products = mm(env[...], rows, ((1,), (1,)), None) * desc ** (-0.5)
        squared = products * products
        kernel = (scale * squared * squared).astype(BF16)
        return mm(selector, kernel, ((1,), (0,)), None) * weight

    head = equations(head_points[...], head_scale[...])
    gram = mm(head, head, ((0,), (0,)))
    for p in range(owners):
        gram_out[p] = gram[p * grow:(p + 1) * grow]
    start, end, _ = exchange(
        lambda to: gram_out.at[to], lambda sender: gram_in.at[sender], g_send, g_recv
    )
    lax.fori_loop(1, owners, start, 0)
    gram_in[me] = gram_out[me]

    outs = []

    def unit_matrix(u):
        loads[u].wait()
        cols = slice(u * unit_cols, (u + 1) * unit_cols)
        matrix[u] = equations(points[u], scale_ref[:, cols])
        out = pltpu.make_async_copy(matrix.at[u], matrix_hbm.at[u], out_sem.at[0, u])
        out.start()
        outs.append(out)

    for u in range(units // 2):
        unit_matrix(u)
    lax.fori_loop(1, owners, end, 0)
    total = gram_in[0]
    for p in range(1, owners):
        total = total + gram_in[p]
    gram_sum[...] = total
    start, end, _ = exchange(
        lambda to: gram_sum, lambda sender: gram_all.at[sender], h_send, h_recv
    )
    lax.fori_loop(1, owners, start, 0)
    gram_all[me] = total
    for u in range(units // 2, units):
        unit_matrix(u)
    lax.fori_loop(1, owners, end, 0)
    gram = jnp.concatenate([gram_all[p] for p in range(owners)], axis=0)

    ridge = ridge_ref[...]
    up1, inv1, shift = factor(gram[:PW, :PW], ridge)
    c12 = mm(inv1, gram[:PW, PW:], ((1,), (0,)))
    back = mm(inv1, c12, ((0,), (0,)))
    pair = jnp.concatenate([c12, jnp.sqrt(shift) * back], axis=0)
    up2, inv2, _ = factor(gram[PW:, PW:] - mm(pair, pair, ((0,), (0,))), ridge)
    q1 = mm(head[:, :PW], inv1, ((1,), (1,)))
    q2 = mm(head[:, PW:] - mm(q1, c12, ((1,), (0,))), inv2, ((1,), (1,)))
    deep = c12 + shift * mm(inv1, back, ((1,), (0,)))
    w2 = mm(head[:, PW:] - mm(q1, deep, ((1,), (0,))), inv2, ((1,), (1,)))
    q_ref[...] = jnp.concatenate([q1, q2], axis=1)
    r_head_ref[...] = jnp.concatenate(
        [
            jnp.concatenate([up1, c12], axis=1),
            jnp.concatenate([jnp.zeros((PW, PW), F32), up2], axis=1),
        ],
        axis=0,
    )
    w_high, w_low = split_bf16(jnp.concatenate([q1, w2], axis=1).T)
    w_wide = jnp.concatenate([w_high, w_low, w_high], axis=1)

    rank = me // 4

    def bit(u, t):
        return (t + u) % 2

    def start_of(u, t):
        return sum(
            (bit_of(me, bit(u, i)) * (owners >> (i + 1)) for i in range(t)), jnp.int32(0)
        )

    def peer(u, t):
        return me + (1 - 2 * bit_of(me, bit(u, t))) * (1 << bit(u, t))

    def reduce_copy(u, t):
        half = owners >> (t + 1)
        first = start_of(u, t) + (1 - bit_of(me, bit(u, t))) * half
        return pltpu.make_async_remote_copy(
            src_ref=sent.at[u, pl.ds(first, half)],
            dst_ref=got.at[u, pl.ds(owners - 2 * half, half)],
            send_sem=r_send.at[u, t], recv_sem=r_recv.at[u, t],
            device_id={"rows": peer(u, t)}, device_id_type=MESH,
        )

    def gather_copy(u, t):
        half = owners >> (t + 1)
        part = whole.at[u, pl.ds(start_of(u, t + 1), half)]
        return pltpu.make_async_remote_copy(
            src_ref=part, dst_ref=part, send_sem=r_send.at[u, 2 + t],
            recv_sem=r_recv.at[u, 2 + t], device_id={"rows": peer(u, t)}, device_id_type=MESH,
        )

    def line_reduce(u, to, sender):
        return pltpu.make_async_remote_copy(
            src_ref=sent.at[u, start_of(u, 2) + to], dst_ref=spot.at[u, sender],
            send_sem=r_send.at[u, 4 + to], recv_sem=r_recv.at[u, 4 + sender],
            device_id={"rows": to * 4 + me % 4}, device_id_type=MESH,
        )

    def line_gather(u, to, sender):
        part = whole.at[u, start_of(u, 2) + sender]
        return pltpu.make_async_remote_copy(
            src_ref=part, dst_ref=part, send_sem=r_send.at[u, 4 + line + to],
            recv_sem=r_recv.at[u, 4 + line + sender],
            device_id={"rows": to * 4 + me % 4}, device_id_type=MESH,
        )

    def others():
        return [(rank + d) % line for d in range(1, line)]

    def open_unit(u):
        m_high, m_low = split_bf16(matrix[u])
        part = mm(
            w_wide, jnp.concatenate([m_high, m_high, m_low], axis=0), ((1,), (0,)), None
        )
        for p in range(owners):
            r, c = (p % row_parts) * high, (p // row_parts) * LANES
            piece = part[r:r + high, c:c + LANES]
            acc[u, p] = piece
            sent[u, p] = piece.astype(BF16)
        reduce_copy(u, 0).start()

    def reduce_step(u, t):
        reduce_copy(u, t).wait_recv()
        half = owners >> (t + 1)
        keep = pl.ds(start_of(u, t + 1), half)
        value = acc[u, keep] + got[u, pl.ds(owners - 2 * half, half)].astype(F32)
        acc[u, keep] = value
        sent[u, keep] = value.astype(BF16)
        if t == 0:
            reduce_copy(u, 1).start()
        else:
            for to in others():
                line_reduce(u, to, rank).start()

    def line_step(u):
        mine_at = start_of(u, 2) + rank
        value = acc[u, mine_at]
        for other in others():
            line_reduce(u, other, other).wait_recv()
            value = value + spot[u, other].astype(F32)
        whole[u, mine_at] = value.astype(BF16)
        for to in others():
            line_gather(u, to, rank).start()

    def line_end(u):
        for other in others():
            line_gather(u, other, other).wait_recv()
        gather_copy(u, 1).start()

    def gather_step(u, t):
        gather_copy(u, t).wait_recv()
        if t:
            gather_copy(u, 0).start()
        else:
            out = pltpu.make_async_copy(whole.at[u], coupled_hbm.at[u], out_sem.at[1, u])
            out.start()
            outs.append(out)

    steps = (
        open_unit, lambda u: reduce_step(u, 0), lambda u: reduce_step(u, 1), line_step, line_end,
        lambda u: gather_step(u, 1), lambda u: gather_step(u, 0),
    )
    plan = sorted(
        (s + LAG * (u // 2), u, s) for u in range(units) for s in range(len(steps))
    )
    for _, u, s in plan:
        steps[s](u)

    for u in range(units):
        for t in range(2):
            reduce_copy(u, t).wait_send()
            gather_copy(u, t).wait_send()
        for to in others():
            line_reduce(u, to, rank).wait_send()
            line_gather(u, to, rank).wait_send()
    for out in outs:
        out.wait()

    def drain(d, _):
        other = (me + d) % owners
        routed(other, other).wait_send()
        return 0

    lax.fori_loop(1, owners, drain, 0)

    def drain_pass(i, _):
        pass_on(i % owners, (core + 1 + i // owners) % cores, core).wait_send()
        return 0

    lax.fori_loop(0, owners * (cores - 1), drain_pass, 0)


def fit(descriptors, owner, struct, points, scale, row_weight, ridge, owners, cores, units, capacity):
    col_count, desc = points.shape
    unit_cols = col_count // units
    eq_count = row_weight.shape[0]
    high = unit_cols // owners
    grow = WIDE // owners
    left = capacity % 8
    tail = 0 < left <= 4
    groups = capacity // 8 + (left > 4)
    span = groups * desc + (desc // 2 if tail else 0) + LANES
    env_count = cores * owners * (8 * groups + 4 * tail)
    line = owners // 4
    vmem = pl.BlockSpec(memory_space=pltpu.VMEM)
    hbm = pl.BlockSpec(memory_space=pl.ANY)
    dma = pltpu.SemaphoreType.DMA
    return pl.pallas_call(
        functools.partial(fit_kernel, owners, cores, units, groups, tail),
        out_shape=(
            jax.ShapeDtypeStruct((units, owners, high, LANES), BF16),
            jax.ShapeDtypeStruct((units, eq_count, unit_cols), F32),
            jax.ShapeDtypeStruct((eq_count, WIDE), F32),
            jax.ShapeDtypeStruct((WIDE, WIDE), F32),
        ),
        in_specs=[vmem, vmem, vmem, hbm, vmem, vmem, vmem],
        out_specs=(hbm, hbm, vmem, vmem),
        scratch_shapes=[
            pltpu.VMEM((units, unit_cols, desc), BF16),
            pltpu.VMEM((WIDE, desc), BF16),
            pltpu.VMEM((1, WIDE), F32),
            pltpu.VMEM((2, owner.shape[0], LANES), F32),
            pltpu.VMEM((owners, 8, span), BF16),
            pltpu.VMEM((cores, owners, 8, span), BF16),
            pltpu.VMEM((env_count, desc), BF16),
            pltpu.VMEM((units, eq_count, unit_cols), F32),
            pltpu.VMEM((owners, grow, WIDE), F32),
            pltpu.VMEM((owners, grow, WIDE), F32),
            pltpu.VMEM((grow, WIDE), F32),
            pltpu.VMEM((owners, grow, WIDE), F32),
            pltpu.VMEM((units, owners, high, LANES), F32),
            pltpu.VMEM((units, owners, high, LANES), BF16),
            pltpu.VMEM((units, owners, high, LANES), BF16),
            pltpu.VMEM((units, line, high, LANES), BF16),
            pltpu.VMEM((units, owners, high, LANES), BF16),
            dma((units,)),
            dma((2, units)),
            dma,
            dma((2, cores)),
            dma((2,)),
            dma((owners,)),
            dma((owners,)),
            dma((cores, owners)),
            dma((cores, owners)),
            dma((owners,)),
            dma((owners,)),
            dma((owners,)),
            dma((owners,)),
            dma((units, 4 + 2 * line)),
            dma((units, 4 + 2 * line)),
        ],
        compiler_params=pltpu.CompilerParams(collective_id=0, has_side_effects=True),
    )(
        descriptors, owner.reshape(1, -1), struct.reshape(1, -1), points, scale.reshape(1, -1),
        row_weight.reshape(1, -1), ridge.reshape(1, 1),
    )


def finish_kernel(norm_scale, coupled_ref, matrix_ref, q_ref, r_head_ref, r_ref, reduced_ref):
    units, owners, high, _ = coupled_ref.shape
    unit_cols = matrix_ref.shape[2]
    row_parts = WIDE // high
    q_cols = q_ref[...]
    q_high, q_low = split_bf16(q_cols)
    q_wide = jnp.concatenate([q_high, q_low], axis=1)
    for u in range(units):
        cols = [
            jnp.concatenate(
                [coupled_ref[u, c * row_parts + r] for r in range(row_parts)], axis=0
            )
            for c in range(owners // row_parts)
        ]
        coupled = jnp.concatenate(cols, axis=1)
        update = mm(q_wide, jnp.concatenate([coupled, coupled], axis=0), ((1,), (0,)), None)
        at = slice(u * unit_cols, (u + 1) * unit_cols)
        r_ref[:, at] = coupled.astype(F32) * norm_scale
        reduced_ref[:, at] = matrix_ref[u] - update

    @pl.when((lax.axis_index("cols") == 0) & (pl.program_id(0) == 0))
    def _():
        r_ref[:, :WIDE] = r_head_ref[...] * norm_scale
        reduced_ref[:, :WIDE] = q_cols


def finish(coupled, matrix, q_cols, r_head, norm_scale):
    units, owners, high, _ = coupled.shape
    _, eq_count, unit_cols = matrix.shape
    each = max(1, units // 2)
    return pl.pallas_call(
        functools.partial(finish_kernel, norm_scale),
        grid=(units // each,),
        out_shape=(
            jax.ShapeDtypeStruct((WIDE, units * unit_cols), F32),
            jax.ShapeDtypeStruct((eq_count, units * unit_cols), F32),
        ),
        in_specs=[
            pl.BlockSpec((each, owners, high, LANES), lambda u: (u, 0, 0, 0)),
            pl.BlockSpec((each, eq_count, unit_cols), lambda u: (u, 0, 0)),
            pl.BlockSpec((eq_count, WIDE), lambda u: (0, 0)),
            pl.BlockSpec((WIDE, WIDE), lambda u: (0, 0)),
        ],
        out_specs=(
            pl.BlockSpec((WIDE, each * unit_cols), lambda u: (0, u)),
            pl.BlockSpec((eq_count, each * unit_cols), lambda u: (0, u)),
        ),
    )(coupled, matrix, q_cols, r_head)


def body(
    descriptors, sparse_points, point_scale, env_owner, env_structure, row_weight, ridge_factor
):
    owners, cores = lax.axis_size("rows"), lax.axis_size("cols")
    eq_count = row_weight.shape[0]
    env_local = descriptors.shape[0]
    col_count = sparse_points.shape[0]
    per_block = max(2, (3 * BLOCK + 2 * owners - 1) // (2 * owners))
    capacity = min(env_local, per_block * (-(-env_local // BLOCK)))
    units = max(1, min(UNITS, col_count // (16 * owners)))
    coupled, matrix, q_cols, r_head = fit(
        descriptors, env_owner, env_structure, sparse_points, point_scale, row_weight,
        ridge_factor, owners, cores, units, capacity,
    )
    return finish(coupled, matrix, q_cols, r_head, 1.0 / math.sqrt(owners * eq_count))


def solution(mesh):
    return jax.shard_map(
        body,
        mesh=mesh,
        in_specs=(
            P(("rows", "cols"), None),
            P("cols", None),
            P("cols"),
            P("rows", None),
            P("rows"),
            P("rows"),
            P(),
        ),
        out_specs=(P(None, "cols"), P("rows", "cols")),
        check_vma=False,
    )
```

time: 109 us -> 73.6 us (0.68)
  starting transfers between devices: 8.34 us -> 0 us
  local copies, waits for them, and re-layouts: 7.55 us -> 0 us
  waiting for transfers between devices: 7.29 us -> 0 us
  blocking collectives: 6.42 us -> 0 us
  Pallas kernels: 74.2 us -> 72.2 us
  other arithmetic: 1.83 us -> 0 us
  matrix products: 1.22 us -> 0 us
    all_to_all x1 -> x0, starting transfers between devices: 8.34 us -> none  [body(): arrived = lax.all_to_all(payload, 'rows', 0, 0, tiled=True)]
    all_to_all x1 -> x0, waiting for transfers between devices: 7.29 us -> none  [body(): arrived = lax.all_to_all(payload, 'rows', 0, 0, tiled=True)]
    all_gather x3 -> x0, blocking collectives: 6.42 us -> none  [the longest x2 3.98 us: from_root(): return lax.all_gather(value, axis)[0]]
    slice x4 -> x0, local copies, waits for them, and re-layouts: 3.26 us -> none  [the longest x2 1.3 us: from_root(): return lax.all_gather(value, axis)[0]]
    pallas_call x2, Pallas kernels: 74.2 us -> 72.2 us  [the longest x1 69 us: fit(): pl.pallas_call(functools.partial(fit_kernel, owners, cores, units, groups...]
    add x2 -> x0, other arithmetic: 1.42 us -> none  [the longest x1 0.76 us: body(): tag = jnp.where(lane == 0, struct[:, None] + 1, 0).astype(BF16)]
    reshape x1 -> x0, local copies, waits for them, and re-layouts: 1.35 us -> none  [fit(): row_weight.reshape(-1, 1)]
    dot_general x1 -> x0, matrix products: 1.22 us -> none  [mm(): lax.dot_general(left, right, ((contract[0], contract[1]), ((), ())), prec...]
  transfers between devices with their start and end apart: 1 -> 0, of which waited for: 1 -> 0; matrix products, arithmetic and copies ran while one was open for 4% -> 0% of each run, Pallas kernels for 0% -> 0%
where the time goes in v2:
time: 73.6 us; the launch traced here: 73.4 us
  Pallas kernels  72.2 us (98%)
  between operations  1.29 us (2%)
    pallas_call x1, Pallas kernels, fit(): pl.pallas_call(functools.partial(fit_kernel, owners, cores, units, groups...  69 us
    pallas_call x1, Pallas kernels, finish(): pl.pallas_call(functools.partial(finish_kernel, norm_scale), grid=(units...  3.18 us

profile of v2, /device:TPU:0, one launch (start us, length us, event | category | flops | bytes accessed | tf_op | source)
XLA Modules:
  0.0 73.4 jit_solution(14907901791561220924)
XLA Ops:
  1.3 69.0 %shard_map.86 = (bf16[4,16,64,128]{3,2,1,0:T(8,128)(2,1)}, f32[4,64,1024]{2,1,0:T(8,128)}, f32[64,128]{1,0:T(8,128)}, f32[128,128]{1,0:T(8,128)}) custom-call(bf16[128,1024]{1,0:T(8,128)(2,1)} %desc_ref.1, s32[1,256]{1,0:T(1,128)} %bitcast.7, s32[1,256]{1,0:T(1,128)} %bitcast.8, bf16[4096,1024]{1,0:T(8,128)(2,1)} %points_hbm.1, f32[1,4096]{1,0:T(1,128)} %bitcast.6, ...), custom_call_target="tpu_custom_call" | custom-call | tf_op jit(solution)/shard_map/pallas_call | solution.py:509
  70.3 3.2 %shard_map.87 = (f32[128,4096]{1,0:T(8,128)}, f32[64,4096]{1,0:T(8,128)}) custom-call(bf16[4,16,64,128]{3,2,1,0:T(8,128)(2,1)} %get-tuple-element.6.coupled_ref, f32[4,64,1024]{2,1,0:T(8,128)} %get-tuple-element.7.matrix_ref, f32[64,128]{1,0:T(8,128)} %get-tuple-element.8.q_ref, f32[128,128]{1,0:T(8,128)} %get-tuple-element.9.r_head_ref), custom_call_target="tpu_custom_call" | custom-call | tf_op jit(solution)/shard_map/pallas_call | solution.py:590

commit v3 on v2

--- a/solution.py
+++ b/solution.py
@@ -14,8 +14,7 @@
 BLOCK = 128
 LANES = 128
 PIVOTS = 8
-UNITS = 4
-LAG = 0.3
+UNITS = 2
 HI = lax.Precision.HIGHEST
 F32 = jnp.float32
 BF16 = jnp.bfloat16
@@ -78,9 +77,9 @@
     desc_ref, owner_ref, struct_ref, points_hbm, scale_ref, weight_ref, ridge_ref,
     coupled_hbm, matrix_hbm, q_ref, r_head_ref,
     points, head_points, head_scale, keys, parcel, landed, env, matrix,
-    gram_out, gram_in, gram_sum, gram_all, acc, sent, got, spot, whole,
+    head_out, heads, block_out, block_in, whole,
     points_sem, out_sem, root_sem, root_send, root_recv, e_send, e_recv, f_send, f_recv,
-    g_send, g_recv, h_send, h_recv, r_send, r_recv,
+    h_send, h_recv, k_send, k_recv, b_send, b_recv, r_send, r_recv,
 ):
     me = lax.axis_index("rows")
     core = lax.axis_index("cols")
@@ -88,9 +87,9 @@
     eq_count = weight_ref.shape[1]
     col_count = scale_ref.shape[1]
     unit_cols = col_count // units
-    grow = WIDE // owners
-    high = unit_cols // owners
-    row_parts = WIDE // high
+    width = unit_cols // owners
+    lanes = block_in.shape[3]
+    share = eq_count // cores
     line = owners // 4
     half_desc = desc // 2
 
@@ -302,52 +301,137 @@
         return mm(selector, kernel, ((1,), (0,)), None) * weight
 
     head = equations(head_points[...], head_scale[...])
-    gram = mm(head, head, ((0,), (0,)))
-    for p in range(owners):
-        gram_out[p] = gram[p * grow:(p + 1) * grow]
-    start, end, _ = exchange(
-        lambda to: gram_out.at[to], lambda sender: gram_in.at[sender], g_send, g_recv
+    for c in range(cores):
+        head_out[c] = head[c * share:(c + 1) * share]
+    start, _, shared = exchange(
+        lambda to: head_out.at[core], lambda sender: heads.at[sender, core], h_send, h_recv
     )
     lax.fori_loop(1, owners, start, 0)
-    gram_in[me] = gram_out[me]
+    heads[me] = head_out[...]
 
     outs = []
-
-    def unit_matrix(u):
+    blocks = []
+    for u in range(units):
         loads[u].wait()
-        cols = slice(u * unit_cols, (u + 1) * unit_cols)
-        matrix[u] = equations(points[u], scale_ref[:, cols])
+        value = equations(points[u], scale_ref[:, u * unit_cols:(u + 1) * unit_cols])
+        matrix[u] = value
         out = pltpu.make_async_copy(matrix.at[u], matrix_hbm.at[u], out_sem.at[0, u])
         out.start()
         outs.append(out)
-
-    for u in range(units // 2):
-        unit_matrix(u)
-    lax.fori_loop(1, owners, end, 0)
-    total = gram_in[0]
-    for p in range(1, owners):
-        total = total + gram_in[p]
-    gram_sum[...] = total
-    start, end, _ = exchange(
-        lambda to: gram_sum, lambda sender: gram_all.at[sender], h_send, h_recv
-    )
-    lax.fori_loop(1, owners, start, 0)
-    gram_all[me] = total
-    for u in range(units // 2, units):
-        unit_matrix(u)
-    lax.fori_loop(1, owners, end, 0)
-    gram = jnp.concatenate([gram_all[p] for p in range(owners)], axis=0)
-
+        value = value.astype(BF16)
+        for p in range(owners):
+            block_out[u, p, :, :width] = value[:, p * width:(p + 1) * width]
+        start, end, _ = exchange(
+            lambda to, u=u: block_out.at[u, to], lambda sender, u=u: block_in.at[u, sender],
+            b_send.at[u], b_recv.at[u],
+        )
+        lax.fori_loop(1, owners, start, 0)
+        block_in[u, me] = block_out[u, me]
+        blocks.append(end)
+
+    def hand_head(slot, to, sender):
+        part = heads.at[slot, sender]
+        return pltpu.make_async_remote_copy(
+            src_ref=part, dst_ref=part, send_sem=k_send.at[to, slot],
+            recv_sem=k_recv.at[sender, slot], device_id={"cols": to}, device_id_type=MESH,
+        )
+
+    def land_head(d, _):
+        other = (me + d) % owners
+        shared(other, other).wait_recv()
+
+        def one(e, _):
+            hand_head(other, (core + e) % cores, core).start()
+            return 0
+
+        lax.fori_loop(1, cores, one, 0)
+        return 0
+
+    lax.fori_loop(1, owners, land_head, 0)
+
+    def handed(i, _):
+        other = (core + 1 + i // (owners - 1)) % cores
+        hand_head((me + 1 + i % (owners - 1)) % owners, other, other).wait_recv()
+        return 0
+
+    lax.fori_loop(0, (owners - 1) * (cores - 1), handed, 0)
+
+    every = heads[...].reshape(owners * eq_count, WIDE)
+    gram = mm(every, every, ((0,), (0,)))
     ridge = ridge_ref[...]
     up1, inv1, shift = factor(gram[:PW, :PW], ridge)
+
+    rank = me // 4
+
+    def bit(u, t):
+        return (t + u) % 2
+
+    def start_of(u, t):
+        return sum(
+            (bit_of(me, bit(u, i)) * (owners >> (i + 1)) for i in range(t)), jnp.int32(0)
+        )
+
+    def gather_copy(u, k, t):
+        half = owners >> (t + 1)
+        part = whole.at[u, k, pl.ds(start_of(u, t + 1), half)]
+        to = me + (1 - 2 * bit_of(me, bit(u, t))) * (1 << bit(u, t))
+        return pltpu.make_async_remote_copy(
+            src_ref=part, dst_ref=part, send_sem=r_send.at[u, k, t],
+            recv_sem=r_recv.at[u, k, t], device_id={"rows": to}, device_id_type=MESH,
+        )
+
+    def line_copy(u, k, to, sender):
+        part = whole.at[u, k, start_of(u, 2) + sender]
+        return pltpu.make_async_remote_copy(
+            src_ref=part, dst_ref=part, send_sem=r_send.at[u, k, 2 + to],
+            recv_sem=r_recv.at[u, k, 2 + sender],
+            device_id={"rows": to * 4 + me % 4}, device_id_type=MESH,
+        )
+
+    others = [(rank + d) % line for d in range(1, line)]
+
+    def open_piece(u, k, value):
+        whole[u, k, start_of(u, 2) + rank] = value.astype(BF16)
+        for to in others:
+            line_copy(u, k, to, rank).start()
+
+    def line_end(u, k):
+        for other in others:
+            line_copy(u, k, other, other).wait_recv()
+        gather_copy(u, k, 1).start()
+
+    def middle(u, k):
+        gather_copy(u, k, 1).wait_recv()
+        gather_copy(u, k, 0).start()
+
+    def last(u, k):
+        gather_copy(u, k, 0).wait_recv()
+        out = pltpu.make_async_copy(whole.at[u, k], coupled_hbm.at[u, k], out_sem.at[1 + k, u])
+        out.start()
+        outs.append(out)
+
+    crosses, firsts = [], []
+    for u in range(units):
+        lax.fori_loop(1, owners, blocks[u], 0)
+        cross = mm(
+            every, block_in[u].reshape(owners * eq_count, lanes).astype(F32), ((0,), (0,))
+        )
+        first = mm(inv1, cross[:PW], ((1,), (0,)))
+        open_piece(u, 0, first)
+        crosses.append(cross)
+        firsts.append(first)
+
     c12 = mm(inv1, gram[:PW, PW:], ((1,), (0,)))
     back = mm(inv1, c12, ((0,), (0,)))
     pair = jnp.concatenate([c12, jnp.sqrt(shift) * back], axis=0)
+    deep = c12 + shift * mm(inv1, back, ((1,), (0,)))
     up2, inv2, _ = factor(gram[PW:, PW:] - mm(pair, pair, ((0,), (0,))), ridge)
+    for u in range(units):
+        rest = crosses[u][PW:] - mm(deep, firsts[u], ((0,), (0,)))
+        open_piece(u, 1, mm(inv2, rest, ((1,), (0,))))
+
     q1 = mm(head[:, :PW], inv1, ((1,), (1,)))
     q2 = mm(head[:, PW:] - mm(q1, c12, ((1,), (0,))), inv2, ((1,), (1,)))
-    deep = c12 + shift * mm(inv1, back, ((1,), (0,)))
-    w2 = mm(head[:, PW:] - mm(q1, deep, ((1,), (0,))), inv2, ((1,), (1,)))
     q_ref[...] = jnp.concatenate([q1, q2], axis=1)
     r_head_ref[...] = jnp.concatenate(
         [
@@ -356,130 +440,30 @@
         ],
         axis=0,
     )
-    w_high, w_low = split_bf16(jnp.concatenate([q1, w2], axis=1).T)
-    w_wide = jnp.concatenate([w_high, w_low, w_high], axis=1)
-
-    rank = me // 4
-
-    def bit(u, t):
-        return (t + u) % 2
-
-    def start_of(u, t):
-        return sum(
-            (bit_of(me, bit(u, i)) * (owners >> (i + 1)) for i in range(t)), jnp.int32(0)
-        )
-
-    def peer(u, t):
-        return me + (1 - 2 * bit_of(me, bit(u, t))) * (1 << bit(u, t))
-
-    def reduce_copy(u, t):
-        half = owners >> (t + 1)
-        first = start_of(u, t) + (1 - bit_of(me, bit(u, t))) * half
-        return pltpu.make_async_remote_copy(
-            src_ref=sent.at[u, pl.ds(first, half)],
-            dst_ref=got.at[u, pl.ds(owners - 2 * half, half)],
-            send_sem=r_send.at[u, t], recv_sem=r_recv.at[u, t],
-            device_id={"rows": peer(u, t)}, device_id_type=MESH,
-        )
-
-    def gather_copy(u, t):
-        half = owners >> (t + 1)
-        part = whole.at[u, pl.ds(start_of(u, t + 1), half)]
-        return pltpu.make_async_remote_copy(
-            src_ref=part, dst_ref=part, send_sem=r_send.at[u, 2 + t],
-            recv_sem=r_recv.at[u, 2 + t], device_id={"rows": peer(u, t)}, device_id_type=MESH,
-        )
-
-    def line_reduce(u, to, sender):
-        return pltpu.make_async_remote_copy(
-            src_ref=sent.at[u, start_of(u, 2) + to], dst_ref=spot.at[u, sender],
-            send_sem=r_send.at[u, 4 + to], recv_sem=r_recv.at[u, 4 + sender],
-            device_id={"rows": to * 4 + me % 4}, device_id_type=MESH,
-        )
-
-    def line_gather(u, to, sender):
-        part = whole.at[u, start_of(u, 2) + sender]
-        return pltpu.make_async_remote_copy(
-            src_ref=part, dst_ref=part, send_sem=r_send.at[u, 4 + line + to],
-            recv_sem=r_recv.at[u, 4 + line + sender],
-            device_id={"rows": to * 4 + me % 4}, device_id_type=MESH,
-        )
-
-    def others():
-        return [(rank + d) % line for d in range(1, line)]
-
-    def open_unit(u):
-        m_high, m_low = split_bf16(matrix[u])
-        part = mm(
-            w_wide, jnp.concatenate([m_high, m_high, m_low], axis=0), ((1,), (0,)), None
-        )
-        for p in range(owners):
-            r, c = (p % row_parts) * high, (p // row_parts) * LANES
-            piece = part[r:r + high, c:c + LANES]
-            acc[u, p] = piece
-            sent[u, p] = piece.astype(BF16)
-        reduce_copy(u, 0).start()
-
-    def reduce_step(u, t):
-        reduce_copy(u, t).wait_recv()
-        half = owners >> (t + 1)
-        keep = pl.ds(start_of(u, t + 1), half)
-        value = acc[u, keep] + got[u, pl.ds(owners - 2 * half, half)].astype(F32)
-        acc[u, keep] = value
-        sent[u, keep] = value.astype(BF16)
-        if t == 0:
-            reduce_copy(u, 1).start()
-        else:
-            for to in others():
-                line_reduce(u, to, rank).start()
-
-    def line_step(u):
-        mine_at = start_of(u, 2) + rank
-        value = acc[u, mine_at]
-        for other in others():
-            line_reduce(u, other, other).wait_recv()
-            value = value + spot[u, other].astype(F32)
-        whole[u, mine_at] = value.astype(BF16)
-        for to in others():
-            line_gather(u, to, rank).start()
-
-    def line_end(u):
-        for other in others():
-            line_gather(u, other, other).wait_recv()
-        gather_copy(u, 1).start()
-
-    def gather_step(u, t):
-        gather_copy(u, t).wait_recv()
-        if t:
-            gather_copy(u, 0).start()
-        else:
-            out = pltpu.make_async_copy(whole.at[u], coupled_hbm.at[u], out_sem.at[1, u])
-            out.start()
-            outs.append(out)
-
-    steps = (
-        open_unit, lambda u: reduce_step(u, 0), lambda u: reduce_step(u, 1), line_step, line_end,
-        lambda u: gather_step(u, 1), lambda u: gather_step(u, 0),
-    )
-    plan = sorted(
-        (s + LAG * (u // 2), u, s) for u in range(units) for s in range(len(steps))
-    )
-    for _, u, s in plan:
-        steps[s](u)
+
+    for k in range(PANELS):
+        for u in range(units):
+            line_end(u, k)
+    for k in range(PANELS):
+        for u in range(units):
+            middle(u, k)
+    for k in range(PANELS):
+        for u in range(units):
+            last(u, k)
 
     for u in range(units):
-        for t in range(2):
-            reduce_copy(u, t).wait_send()
-            gather_copy(u, t).wait_send()
-        for to in others():
-            line_reduce(u, to, rank).wait_send()
-            line_gather(u, to, rank).wait_send()
+        for k in range(PANELS):
+            for t in range(2):
+                gather_copy(u, k, t).wait_send()
+            for to in others:
+                line_copy(u, k, to, rank).wait_send()
     for out in outs:
         out.wait()
 
     def drain(d, _):
         other = (me + d) % owners
         routed(other, other).wait_send()
+        shared(other, other).wait_send()
         return 0
 
     lax.fori_loop(1, owners, drain, 0)
@@ -489,14 +473,20 @@
         return 0
 
     lax.fori_loop(0, owners * (cores - 1), drain_pass, 0)
+
+    def drain_head(i, _):
+        to = (core + 1 + i // (owners - 1)) % cores
+        hand_head((me + 1 + i % (owners - 1)) % owners, to, core).wait_send()
+        return 0
+
+    lax.fori_loop(0, (owners - 1) * (cores - 1), drain_head, 0)
 
 
 def fit(descriptors, owner, struct, points, scale, row_weight, ridge, owners, cores, units, capacity):
     col_count, desc = points.shape
     unit_cols = col_count // units
     eq_count = row_weight.shape[0]
-    high = unit_cols // owners
-    grow = WIDE // owners
+    lanes = max(LANES, unit_cols // owners)
     left = capacity % 8
     tail = 0 < left <= 4
     groups = capacity // 8 + (left > 4)
@@ -509,7 +499,7 @@
     return pl.pallas_call(
         functools.partial(fit_kernel, owners, cores, units, groups, tail),
         out_shape=(
-            jax.ShapeDtypeStruct((units, owners, high, LANES), BF16),
+            jax.ShapeDtypeStruct((units, PANELS, owners, PW, lanes), BF16),
             jax.ShapeDtypeStruct((units, eq_count, unit_cols), F32),
             jax.ShapeDtypeStruct((eq_count, WIDE), F32),
             jax.ShapeDtypeStruct((WIDE, WIDE), F32),
@@ -525,17 +515,13 @@
             pltpu.VMEM((cores, owners, 8, span), BF16),
             pltpu.VMEM((env_count, desc), BF16),
             pltpu.VMEM((units, eq_count, unit_cols), F32),
-            pltpu.VMEM((owners, grow, WIDE), F32),
-            pltpu.VMEM((owners, grow, WIDE), F32),
-            pltpu.VMEM((grow, WIDE), F32),
-            pltpu.VMEM((owners, grow, WIDE), F32),
-            pltpu.VMEM((units, owners, high, LANES), F32),
-            pltpu.VMEM((units, owners, high, LANES), BF16),
-            pltpu.VMEM((units, owners, high, LANES), BF16),
-            pltpu.VMEM((units, line, high, LANES), BF16),
-            pltpu.VMEM((units, owners, high, LANES), BF16),
+            pltpu.VMEM((cores, eq_count // cores, WIDE), F32),
+            pltpu.VMEM((owners, cores, eq_count // cores, WIDE), F32),
+            pltpu.VMEM((units, owners, eq_count, lanes), BF16),
+            pltpu.VMEM((units, owners, eq_count, lanes), BF16),
+            pltpu.VMEM((units, PANELS, owners, PW, lanes), BF16),
             dma((units,)),
-            dma((2, units)),
+            dma((1 + PANELS, units)),
             dma,
             dma((2, cores)),
             dma((2,)),
@@ -545,10 +531,12 @@
             dma((cores, owners)),
             dma((owners,)),
             dma((owners,)),
-            dma((owners,)),
-            dma((owners,)),
-            dma((units, 4 + 2 * line)),
-            dma((units, 4 + 2 * line)),
+            dma((cores, owners)),
+            dma((cores, owners)),
+            dma((units, owners)),
+            dma((units, owners)),
+            dma((units, PANELS, 2 + line)),
+            dma((units, PANELS, 2 + line)),
         ],
         compiler_params=pltpu.CompilerParams(collective_id=0, has_side_effects=True),
     )(
@@ -557,52 +545,53 @@
     )
 
 
+def place_of(owner, unit, owners):
+    first, second = unit % 2, (unit + 1) % 2
+    return (
+        (owner >> first) % 2 * (owners // 2) + (owner >> second) % 2 * (owners // 4) + owner // 4
+    )
+
+
 def finish_kernel(norm_scale, coupled_ref, matrix_ref, q_ref, r_head_ref, r_ref, reduced_ref):
-    units, owners, high, _ = coupled_ref.shape
+    units, _, owners, _, _ = coupled_ref.shape
     unit_cols = matrix_ref.shape[2]
-    row_parts = WIDE // high
+    width = unit_cols // owners
     q_cols = q_ref[...]
     q_high, q_low = split_bf16(q_cols)
     q_wide = jnp.concatenate([q_high, q_low], axis=1)
     for u in range(units):
-        cols = [
-            jnp.concatenate(
-                [coupled_ref[u, c * row_parts + r] for r in range(row_parts)], axis=0
-            )
-            for c in range(owners // row_parts)
-        ]
-        coupled = jnp.concatenate(cols, axis=1)
+        coupled = jnp.concatenate(
+            [
+                jnp.concatenate(
+                    [
+                        coupled_ref[u, k, place_of(p, u, owners)][:, :width]
+                        for p in range(owners)
+                    ],
+                    axis=1,
+                )
+                for k in range(PANELS)
+            ],
+            axis=0,
+        )
         update = mm(q_wide, jnp.concatenate([coupled, coupled], axis=0), ((1,), (0,)), None)
         at = slice(u * unit_cols, (u + 1) * unit_cols)
         r_ref[:, at] = coupled.astype(F32) * norm_scale
         reduced_ref[:, at] = matrix_ref[u] - update
 
-    @pl.when((lax.axis_index("cols") == 0) & (pl.program_id(0) == 0))
+    @pl.when(lax.axis_index("cols") == 0)
     def _():
         r_ref[:, :WIDE] = r_head_ref[...] * norm_scale
         reduced_ref[:, :WIDE] = q_cols
 
 
 def finish(coupled, matrix, q_cols, r_head, norm_scale):
-    units, owners, high, _ = coupled.shape
+    units = coupled.shape[0]
     _, eq_count, unit_cols = matrix.shape
-    each = max(1, units // 2)
     return pl.pallas_call(
         functools.partial(finish_kernel, norm_scale),
-        grid=(units // each,),
         out_shape=(
             jax.ShapeDtypeStruct((WIDE, units * unit_cols), F32),
             jax.ShapeDtypeStruct((eq_count, units * unit_cols), F32),
-        ),
-        in_specs=[
-            pl.BlockSpec((each, owners, high, LANES), lambda u: (u, 0, 0, 0)),
-            pl.BlockSpec((each, eq_count, unit_cols), lambda u: (u, 0, 0)),
-            pl.BlockSpec((eq_count, WIDE), lambda u: (0, 0)),
-            pl.BlockSpec((WIDE, WIDE), lambda u: (0, 0)),
-        ],
-        out_specs=(
-            pl.BlockSpec((WIDE, each * unit_cols), lambda u: (0, u)),
-            pl.BlockSpec((eq_count, each * unit_cols), lambda u: (0, u)),
         ),
     )(coupled, matrix, q_cols, r_head)
 
@@ -616,7 +605,7 @@
     col_count = sparse_points.shape[0]
     per_block = max(2, (3 * BLOCK + 2 * owners - 1) // (2 * owners))
     capacity = min(env_local, per_block * (-(-env_local // BLOCK)))
-    units = max(1, min(UNITS, col_count // (16 * owners)))
+    units = max(1, min(UNITS, col_count // (LANES * owners)))
     coupled, matrix, q_cols, r_head = fit(
         descriptors, env_owner, env_structure, sparse_points, point_scale, row_weight,
         ridge_factor, owners, cores, units, capacity,

time: 73.6 us -> 68.2 us (0.927)
  Pallas kernels: 72.2 us -> 66.7 us
    pallas_call x1, Pallas kernels: 69 us -> 63 us  [fit(): pl.pallas_call(functools.partial(fit_kernel, owners, cores, units, groups...]
where the time goes in v3:
time: 68.2 us; the launch traced here: 68 us
  Pallas kernels  66.7 us (98%)
  between operations  1.29 us (2%)
    pallas_call x1, Pallas kernels, fit(): pl.pallas_call(functools.partial(fit_kernel, owners, cores, units, groups...  63 us
    pallas_call x1, Pallas kernels, finish(): pl.pallas_call(functools.partial(finish_kernel, norm_scale), out_shape=(j...  3.69 us

profile of v3, /device:TPU:0, one launch (start us, length us, event | category | flops | bytes accessed | tf_op | source)
XLA Modules:
  0.0 68.0 jit_solution(10887531173600429048)
XLA Ops:
  1.3 63.0 %shard_map.86 = (bf16[2,2,16,64,128]{4,3,2,1,0:T(8,128)(2,1)}, f32[2,64,2048]{2,1,0:T(8,128)}, f32[64,128]{1,0:T(8,128)}, f32[128,128]{1,0:T(8,128)}) custom-call(bf16[128,1024]{1,0:T(8,128)(2,1)} %desc_ref.1, s32[1,256]{1,0:T(1,128)} %bitcast.7, s32[1,256]{1,0:T(1,128)} %bitcast.8, bf16[4096,1024]{1,0:T(8,128)(2,1)} %points_hbm.1, f32[1,4096]{1,0:T(1,128)} %bitcast.6, ...), custom_call_target="tpu_custom_call" | custom-call | tf_op jit(solution)/shard_map/pallas_call | solution.py:499
  64.3 3.7 %shard_map.87 = (f32[128,4096]{1,0:T(8,128)}, f32[64,4096]{1,0:T(8,128)}) custom-call(bf16[2,2,16,64,128]{4,3,2,1,0:T(8,128)(2,1)} %get-tuple-element.6.coupled_ref, f32[2,64,2048]{2,1,0:T(8,128)} %get-tuple-element.7.matrix_ref, f32[64,128]{1,0:T(8,128)} %get-tuple-element.8.q_ref, f32[128,128]{1,0:T(8,128)} %get-tuple-element.9.r_head_ref), custom_call_target="tpu_custom_call" | custom-call | tf_op jit(solution)/shard_map/pallas_call | solution.py:590

commit v4 on v3

--- a/solution.py
+++ b/solution.py
@@ -15,6 +15,8 @@
 LANES = 128
 PIVOTS = 8
 UNITS = 2
+PARTS = 2
+LAG = 0.9
 HI = lax.Precision.HIGHEST
 F32 = jnp.float32
 BF16 = jnp.bfloat16
@@ -302,7 +304,7 @@
 
     head = equations(head_points[...], head_scale[...])
     for c in range(cores):
-        head_out[c] = head[c * share:(c + 1) * share]
+        head_out[c] = head[c * share:(c + 1) * share].astype(BF16)
     start, _, shared = exchange(
         lambda to: head_out.at[core], lambda sender: heads.at[sender, core], h_send, h_recv
     )
@@ -356,80 +358,15 @@
 
     lax.fori_loop(0, (owners - 1) * (cores - 1), handed, 0)
 
-    every = heads[...].reshape(owners * eq_count, WIDE)
-    gram = mm(every, every, ((0,), (0,)))
+    every = heads[...].astype(F32).reshape(owners * eq_count, WIDE).T.astype(BF16)
+    gram = mm(every, every, ((1,), (1,)), None)
     ridge = ridge_ref[...]
     up1, inv1, shift = factor(gram[:PW, :PW], ridge)
-
-    rank = me // 4
-
-    def bit(u, t):
-        return (t + u) % 2
-
-    def start_of(u, t):
-        return sum(
-            (bit_of(me, bit(u, i)) * (owners >> (i + 1)) for i in range(t)), jnp.int32(0)
-        )
-
-    def gather_copy(u, k, t):
-        half = owners >> (t + 1)
-        part = whole.at[u, k, pl.ds(start_of(u, t + 1), half)]
-        to = me + (1 - 2 * bit_of(me, bit(u, t))) * (1 << bit(u, t))
-        return pltpu.make_async_remote_copy(
-            src_ref=part, dst_ref=part, send_sem=r_send.at[u, k, t],
-            recv_sem=r_recv.at[u, k, t], device_id={"rows": to}, device_id_type=MESH,
-        )
-
-    def line_copy(u, k, to, sender):
-        part = whole.at[u, k, start_of(u, 2) + sender]
-        return pltpu.make_async_remote_copy(
-            src_ref=part, dst_ref=part, send_sem=r_send.at[u, k, 2 + to],
-            recv_sem=r_recv.at[u, k, 2 + sender],
-            device_id={"rows": to * 4 + me % 4}, device_id_type=MESH,
-        )
-
-    others = [(rank + d) % line for d in range(1, line)]
-
-    def open_piece(u, k, value):
-        whole[u, k, start_of(u, 2) + rank] = value.astype(BF16)
-        for to in others:
-            line_copy(u, k, to, rank).start()
-
-    def line_end(u, k):
-        for other in others:
-            line_copy(u, k, other, other).wait_recv()
-        gather_copy(u, k, 1).start()
-
-    def middle(u, k):
-        gather_copy(u, k, 1).wait_recv()
-        gather_copy(u, k, 0).start()
-
-    def last(u, k):
-        gather_copy(u, k, 0).wait_recv()
-        out = pltpu.make_async_copy(whole.at[u, k], coupled_hbm.at[u, k], out_sem.at[1 + k, u])
-        out.start()
-        outs.append(out)
-
-    crosses, firsts = [], []
-    for u in range(units):
-        lax.fori_loop(1, owners, blocks[u], 0)
-        cross = mm(
-            every, block_in[u].reshape(owners * eq_count, lanes).astype(F32), ((0,), (0,))
-        )
-        first = mm(inv1, cross[:PW], ((1,), (0,)))
-        open_piece(u, 0, first)
-        crosses.append(cross)
-        firsts.append(first)
-
     c12 = mm(inv1, gram[:PW, PW:], ((1,), (0,)))
     back = mm(inv1, c12, ((0,), (0,)))
     pair = jnp.concatenate([c12, jnp.sqrt(shift) * back], axis=0)
     deep = c12 + shift * mm(inv1, back, ((1,), (0,)))
     up2, inv2, _ = factor(gram[PW:, PW:] - mm(pair, pair, ((0,), (0,))), ridge)
-    for u in range(units):
-        rest = crosses[u][PW:] - mm(deep, firsts[u], ((0,), (0,)))
-        open_piece(u, 1, mm(inv2, rest, ((1,), (0,))))
-
     q1 = mm(head[:, :PW], inv1, ((1,), (1,)))
     q2 = mm(head[:, PW:] - mm(q1, c12, ((1,), (0,))), inv2, ((1,), (1,)))
     q_ref[...] = jnp.concatenate([q1, q2], axis=1)
@@ -441,20 +378,84 @@
         axis=0,
     )
 
-    for k in range(PANELS):
-        for u in range(units):
-            line_end(u, k)
-    for k in range(PANELS):
-        for u in range(units):
-            middle(u, k)
-    for k in range(PANELS):
-        for u in range(units):
-            last(u, k)
+    rank = me // 4
+
+    def bit(u, t):
+        return (t + u) % 2
+
+    def start_of(u, t):
+        return sum(
+            (bit_of(me, bit(u, i)) * (owners >> (i + 1)) for i in range(t)), jnp.int32(0)
+        )
+
+    def quarter_copy(u, k, t, second):
+        quarter = owners // 4
+        own = bit_of(me, bit(u, 1))
+        at = start_of(u, 1) + (1 - own if second else own) * quarter
+        part = whole.at[u, k, pl.ds(at, quarter)]
+        to = me + (1 - 2 * bit_of(me, bit(u, t))) * (1 << bit(u, t))
+        index = 2 * t + second
+        return pltpu.make_async_remote_copy(
+            src_ref=part, dst_ref=part, send_sem=r_send.at[u, k, index],
+            recv_sem=r_recv.at[u, k, index], device_id={"rows": to}, device_id_type=MESH,
+        )
+
+    def gather_copy(u, k, index):
+        return quarter_copy(u, k, (0, 0, 1)[index], (False, True, False)[index])
+
+    def line_copy(u, k, to, sender):
+        part = whole.at[u, k, start_of(u, 2) + sender]
+        return pltpu.make_async_remote_copy(
+            src_ref=part, dst_ref=part, send_sem=r_send.at[u, k, 3 + to],
+            recv_sem=r_recv.at[u, k, 3 + sender],
+            device_id={"rows": to * 4 + me % 4}, device_id_type=MESH,
+        )
+
+    others = [(rank + d) % line for d in range(1, line)]
+
+    def open_piece(u, k, value):
+        whole[u, k, start_of(u, 2) + rank] = value.astype(BF16)
+        for to in others:
+            line_copy(u, k, to, rank).start()
+
+    def open_unit(u):
+        lax.fori_loop(1, owners, blocks[u], 0)
+        block = block_in[u].astype(F32).reshape(owners * eq_count, lanes).astype(BF16)
+        cross = mm(every, block, ((1,), (0,)), None)
+        first = mm(inv1, cross[:PW], ((1,), (0,)))
+        open_piece(u, 0, first)
+        rest = cross[PW:] - mm(deep, first, ((0,), (0,)))
+        open_piece(u, 1, mm(inv2, rest, ((1,), (0,))))
+
+    def line_end(u):
+        for k in range(PANELS):
+            for other in others:
+                line_copy(u, k, other, other).wait_recv()
+            gather_copy(u, k, 2).start()
+            gather_copy(u, k, 0).start()
+
+    def middle(u):
+        for k in range(PANELS):
+            gather_copy(u, k, 2).wait_recv()
+            gather_copy(u, k, 1).start()
+
+    def last(u):
+        for k in range(PANELS):
+            gather_copy(u, k, 0).wait_recv()
+            gather_copy(u, k, 1).wait_recv()
+        out = pltpu.make_async_copy(whole.at[u], coupled_hbm.at[u], out_sem.at[1, u])
+        out.start()
+        outs.append(out)
+
+    steps = (open_unit, line_end, middle, last)
+    plan = sorted((s + LAG * u, u, s) for u in range(units) for s in range(len(steps)))
+    for _, u, s in plan:
+        steps[s](u)
 
     for u in range(units):
         for k in range(PANELS):
-            for t in range(2):
-                gather_copy(u, k, t).wait_send()
+            for index in range(3):
+                gather_copy(u, k, index).wait_send()
             for to in others:
                 line_copy(u, k, to, rank).wait_send()
     for out in outs:
@@ -515,13 +516,13 @@
             pltpu.VMEM((cores, owners, 8, span), BF16),
             pltpu.VMEM((env_count, desc), BF16),
             pltpu.VMEM((units, eq_count, unit_cols), F32),
-            pltpu.VMEM((cores, eq_count // cores, WIDE), F32),
-            pltpu.VMEM((owners, cores, eq_count // cores, WIDE), F32),
+            pltpu.VMEM((cores, eq_count // cores, WIDE), BF16),
+            pltpu.VMEM((owners, cores, eq_count // cores, WIDE), BF16),
             pltpu.VMEM((units, owners, eq_count, lanes), BF16),
             pltpu.VMEM((units, owners, eq_count, lanes), BF16),
             pltpu.VMEM((units, PANELS, owners, PW, lanes), BF16),
             dma((units,)),
-            dma((1 + PANELS, units)),
+            dma((2, units)),
             dma,
             dma((2, cores)),
             dma((2,)),
@@ -535,8 +536,8 @@
             dma((cores, owners)),
             dma((units, owners)),
             dma((units, owners)),
-            dma((units, PANELS, 2 + line)),
-            dma((units, PANELS, 2 + line)),
+            dma((units, PANELS, 3 + line)),
+            dma((units, PANELS, 3 + line)),
         ],
         compiler_params=pltpu.CompilerParams(collective_id=0, has_side_effects=True),
     )(
@@ -552,47 +553,82 @@
     )
 
 
-def finish_kernel(norm_scale, coupled_ref, matrix_ref, q_ref, r_head_ref, r_ref, reduced_ref):
-    units, _, owners, _, _ = coupled_ref.shape
-    unit_cols = matrix_ref.shape[2]
+def finish_kernel(
+    norm_scale, coupled_hbm, matrix_hbm, q_ref, r_head_ref, r_hbm, reduced_hbm,
+    coupled, matrix, r_out, reduced_out, in_sem, out_sem,
+):
+    units, _, owners, _, _ = coupled.shape
+    unit_cols = matrix.shape[2]
     width = unit_cols // owners
+    loads = []
+    for u in range(units):
+        pair = (
+            pltpu.make_async_copy(coupled_hbm.at[u], coupled.at[u], in_sem.at[0, u]),
+            pltpu.make_async_copy(matrix_hbm.at[u], matrix.at[u], in_sem.at[1, u]),
+        )
+        for load in pair:
+            load.start()
+        loads.append(pair)
     q_cols = q_ref[...]
     q_high, q_low = split_bf16(q_cols)
     q_wide = jnp.concatenate([q_high, q_low], axis=1)
+    root = lax.axis_index("cols") == 0
+    part = unit_cols // PARTS
+    stores = []
     for u in range(units):
-        coupled = jnp.concatenate(
-            [
-                jnp.concatenate(
-                    [
-                        coupled_ref[u, k, place_of(p, u, owners)][:, :width]
-                        for p in range(owners)
-                    ],
-                    axis=1,
+        for load in loads[u]:
+            load.wait()
+        for h in range(PARTS):
+            mine = range(h * owners // PARTS, (h + 1) * owners // PARTS)
+            block = jnp.concatenate(
+                [
+                    jnp.concatenate(
+                        [coupled[u, k, place_of(p, u, owners)][:, :width] for p in mine], axis=1
+                    )
+                    for k in range(PANELS)
+                ],
+                axis=0,
+            )
+            update = mm(q_wide, jnp.concatenate([block, block], axis=0), ((1,), (0,)), None)
+            at = slice(u * unit_cols + h * part, u * unit_cols + (h + 1) * part)
+            r_out[:, at] = block.astype(F32) * norm_scale
+            reduced_out[:, at] = matrix[u, :, h * part:(h + 1) * part] - update
+            if u == 0 and h == 0:
+                r_out[:, :WIDE] = jnp.where(root, r_head_ref[...] * norm_scale, r_out[:, :WIDE])
+                reduced_out[:, :WIDE] = jnp.where(root, q_cols, reduced_out[:, :WIDE])
+            for i, (src, dst) in enumerate(((r_out, r_hbm), (reduced_out, reduced_hbm))):
+                store = pltpu.make_async_copy(
+                    src.at[:, at], dst.at[:, at], out_sem.at[i, u * PARTS + h]
                 )
-                for k in range(PANELS)
-            ],
-            axis=0,
-        )
-        update = mm(q_wide, jnp.concatenate([coupled, coupled], axis=0), ((1,), (0,)), None)
-        at = slice(u * unit_cols, (u + 1) * unit_cols)
-        r_ref[:, at] = coupled.astype(F32) * norm_scale
-        reduced_ref[:, at] = matrix_ref[u] - update
-
-    @pl.when(lax.axis_index("cols") == 0)
-    def _():
-        r_ref[:, :WIDE] = r_head_ref[...] * norm_scale
-        reduced_ref[:, :WIDE] = q_cols
+                store.start()
+                stores.append(store)
+    for store in stores:
+        store.wait()
 
 
 def finish(coupled, matrix, q_cols, r_head, norm_scale):
     units = coupled.shape[0]
     _, eq_count, unit_cols = matrix.shape
+    vmem = pl.BlockSpec(memory_space=pltpu.VMEM)
+    hbm = pl.BlockSpec(memory_space=pl.ANY)
+    r_shape = (WIDE, units * unit_cols)
+    reduced_shape = (eq_count, units * unit_cols)
     return pl.pallas_call(
         functools.partial(finish_kernel, norm_scale),
         out_shape=(
-            jax.ShapeDtypeStruct((WIDE, units * unit_cols), F32),
-            jax.ShapeDtypeStruct((eq_count, units * unit_cols), F32),
+            jax.ShapeDtypeStruct(r_shape, F32),
+            jax.ShapeDtypeStruct(reduced_shape, F32),
         ),
+        in_specs=[hbm, hbm, vmem, vmem],
+        out_specs=(hbm, hbm),
+        scratch_shapes=[
+            pltpu.VMEM(coupled.shape, BF16),
+            pltpu.VMEM(matrix.shape, F32),
+            pltpu.VMEM(r_shape, F32),
+            pltpu.VMEM(reduced_shape, F32),
+            pltpu.SemaphoreType.DMA((2, units)),
+            pltpu.SemaphoreType.DMA((2, units * PARTS)),
+        ],
     )(coupled, matrix, q_cols, r_head)
 
 

time: 68.2 us -> 61.5 us (0.902)
  Pallas kernels: 66.7 us -> 60 us
    pallas_call x1, Pallas kernels: 63 us -> 56.1 us  [fit(): pl.pallas_call(functools.partial(fit_kernel, owners, cores, units, groups...]
where the time goes in v4:
time: 61.5 us; the launch traced here: 61.2 us
  Pallas kernels  60 us (98%)
  between operations  1.29 us (2%)
    pallas_call x1, Pallas kernels, fit(): pl.pallas_call(functools.partial(fit_kernel, owners, cores, units, groups...  56.1 us
    pallas_call x1, Pallas kernels, finish(): pl.pallas_call(functools.partial(finish_kernel, norm_scale), out_shape=(j...  3.89 us

profile of v4, /device:TPU:0, one launch (start us, length us, event | category | flops | bytes accessed | tf_op | source)
XLA Modules:
  0.0 61.2 jit_solution(2845809415013799565)
XLA Ops:
  1.3 56.1 %shard_map.86 = (bf16[2,2,16,64,128]{4,3,2,1,0:T(8,128)(2,1)}, f32[2,64,2048]{2,1,0:T(8,128)}, f32[64,128]{1,0:T(8,128)}, f32[128,128]{1,0:T(8,128)}) custom-call(bf16[128,1024]{1,0:T(8,128)(2,1)} %desc_ref.1, s32[1,256]{1,0:T(1,128)} %bitcast.7, s32[1,256]{1,0:T(1,128)} %bitcast.8, bf16[4096,1024]{1,0:T(8,128)(2,1)} %points_hbm.1, f32[1,4096]{1,0:T(1,128)} %bitcast.6, ...), custom_call_target="tpu_custom_call" | custom-call | tf_op jit(solution)/shard_map/pallas_call | solution.py:500
  57.4 3.9 %shard_map.87 = (f32[128,4096]{1,0:T(8,128)}, f32[64,4096]{1,0:T(8,128)}) custom-call(bf16[2,2,16,64,128]{4,3,2,1,0:T(8,128)(2,1)} %get-tuple-element.6.coupled_hbm, f32[2,64,2048]{2,1,0:T(8,128)} %get-tuple-element.7.matrix_hbm, f32[64,128]{1,0:T(8,128)} %get-tuple-element.8.q_ref, f32[128,128]{1,0:T(8,128)} %get-tuple-element.9.r_head_ref), custom_call_target="tpu_custom_call" | custom-call | tf_op jit(solution)/shard_map/pallas_call | solution.py:616

commit v5 on v4

--- a/solution.py
+++ b/solution.py
@@ -17,6 +17,8 @@
 UNITS = 2
 PARTS = 2
 LAG = 0.9
+FIT_VMEM = 44 << 20
+FINISH_VMEM = 16 << 20
 HI = lax.Precision.HIGHEST
 F32 = jnp.float32
 BF16 = jnp.bfloat16
@@ -76,11 +78,12 @@
 
 def fit_kernel(
     owners, cores, units, groups, tail,
-    desc_ref, owner_ref, struct_ref, points_hbm, scale_ref, weight_ref, ridge_ref,
-    coupled_hbm, matrix_hbm, q_ref, r_head_ref,
-    points, head_points, head_scale, keys, parcel, landed, env, matrix,
+    desc_hbm, owner_hbm, struct_hbm, points_hbm, scale_hbm, weight_hbm, ridge_hbm,
+    coupled_ref, matrix_ref, q_ref, r_head_ref,
+    desc_ref, owner_ref, struct_ref, scale_ref, weight_ref, ridge_ref,
+    points, head_points, head_scale, keys, parcel, landed, env,
     head_out, heads, block_out, block_in, whole,
-    points_sem, out_sem, root_sem, root_send, root_recv, e_send, e_recv, f_send, f_recv,
+    start_sem, points_sem, out_sem, root_sem, root_send, root_recv, e_send, e_recv, f_send, f_recv,
     h_send, h_recv, k_send, k_recv, b_send, b_recv, r_send, r_recv,
 ):
     me = lax.axis_index("rows")
@@ -112,6 +115,15 @@
     lax.fori_loop(1, owners, greet_rows, 0)
     lax.fori_loop(1, cores, greet_cols, 0)
 
+    inputs = (
+        (owner_hbm, owner_ref), (struct_hbm, struct_ref), (desc_hbm, desc_ref),
+        (scale_hbm, scale_ref), (weight_hbm, weight_ref), (ridge_hbm, ridge_ref),
+    )
+    inputs = [
+        pltpu.make_async_copy(src, dst, start_sem.at[i]) for i, (src, dst) in enumerate(inputs)
+    ]
+    for load in inputs:
+        load.start()
     loads = []
     for u in range(units):
         load = pltpu.make_async_copy(
@@ -123,6 +135,8 @@
     def as_column(row):
         return jnp.broadcast_to(row.astype(F32), (LANES, row.shape[1])).T
 
+    for load in inputs:
+        load.wait()
     keys[0] = as_column(owner_ref[...])
     keys[1] = as_column(struct_ref[...])
     mine = pl.ds(pl.multiple_of(core * env_local, 8), env_local)
@@ -316,10 +330,7 @@
     for u in range(units):
         loads[u].wait()
         value = equations(points[u], scale_ref[:, u * unit_cols:(u + 1) * unit_cols])
-        matrix[u] = value
-        out = pltpu.make_async_copy(matrix.at[u], matrix_hbm.at[u], out_sem.at[0, u])
-        out.start()
-        outs.append(out)
+        matrix_ref[u] = value
         value = value.astype(BF16)
         for p in range(owners):
             block_out[u, p, :, :width] = value[:, p * width:(p + 1) * width]
@@ -360,7 +371,7 @@
 
     every = heads[...].astype(F32).reshape(owners * eq_count, WIDE).T.astype(BF16)
     gram = mm(every, every, ((1,), (1,)), None)
-    ridge = ridge_ref[...]
+    ridge = ridge_ref[:, :1]
     up1, inv1, shift = factor(gram[:PW, :PW], ridge)
     c12 = mm(inv1, gram[:PW, PW:], ((1,), (0,)))
     back = mm(inv1, c12, ((0,), (0,)))
@@ -443,7 +454,7 @@
         for k in range(PANELS):
             gather_copy(u, k, 0).wait_recv()
             gather_copy(u, k, 1).wait_recv()
-        out = pltpu.make_async_copy(whole.at[u], coupled_hbm.at[u], out_sem.at[1, u])
+        out = pltpu.make_async_copy(whole.at[u], coupled_ref.at[u], out_sem.at[u])
         out.start()
         outs.append(out)
 
@@ -495,7 +506,7 @@
     env_count = cores * owners * (8 * groups + 4 * tail)
     line = owners // 4
     vmem = pl.BlockSpec(memory_space=pltpu.VMEM)
-    hbm = pl.BlockSpec(memory_space=pl.ANY)
+    hbm = pl.BlockSpec(memory_space=pltpu.HBM)
     dma = pltpu.SemaphoreType.DMA
     return pl.pallas_call(
         functools.partial(fit_kernel, owners, cores, units, groups, tail),
@@ -505,9 +516,15 @@
             jax.ShapeDtypeStruct((eq_count, WIDE), F32),
             jax.ShapeDtypeStruct((WIDE, WIDE), F32),
         ),
-        in_specs=[vmem, vmem, vmem, hbm, vmem, vmem, vmem],
-        out_specs=(hbm, hbm, vmem, vmem),
+        in_specs=[hbm] * 7,
+        out_specs=(vmem, vmem, vmem, vmem),
         scratch_shapes=[
+            pltpu.VMEM(descriptors.shape, BF16),
+            pltpu.VMEM((1, owner.shape[0]), jnp.int32),
+            pltpu.VMEM((1, owner.shape[0]), jnp.int32),
+            pltpu.VMEM((1, col_count), F32),
+            pltpu.VMEM((1, eq_count), F32),
+            pltpu.VMEM((1, LANES), F32),
             pltpu.VMEM((units, unit_cols, desc), BF16),
             pltpu.VMEM((WIDE, desc), BF16),
             pltpu.VMEM((1, WIDE), F32),
@@ -515,14 +532,14 @@
             pltpu.VMEM((owners, 8, span), BF16),
             pltpu.VMEM((cores, owners, 8, span), BF16),
             pltpu.VMEM((env_count, desc), BF16),
-            pltpu.VMEM((units, eq_count, unit_cols), F32),
             pltpu.VMEM((cores, eq_count // cores, WIDE), BF16),
             pltpu.VMEM((owners, cores, eq_count // cores, WIDE), BF16),
             pltpu.VMEM((units, owners, eq_count, lanes), BF16),
             pltpu.VMEM((units, owners, eq_count, lanes), BF16),
             pltpu.VMEM((units, PANELS, owners, PW, lanes), BF16),
+            dma((6,)),
             dma((units,)),
-            dma((2, units)),
+            dma((units,)),
             dma,
             dma((2, cores)),
             dma((2,)),
@@ -539,10 +556,18 @@
             dma((units, PANELS, 3 + line)),
             dma((units, PANELS, 3 + line)),
         ],
-        compiler_params=pltpu.CompilerParams(collective_id=0, has_side_effects=True),
+        compiler_params=pltpu.CompilerParams(
+            collective_id=0, has_side_effects=True, vmem_limit_bytes=FIT_VMEM
+        ),
     )(
-        descriptors, owner.reshape(1, -1), struct.reshape(1, -1), points, scale.reshape(1, -1),
-        row_weight.reshape(1, -1), ridge.reshape(1, 1),
+        *(
+            pltpu.with_memory_space_constraint(value, pltpu.HBM)
+            for value in (
+                descriptors, owner.reshape(1, -1), struct.reshape(1, -1), points,
+                scale.reshape(1, -1), row_weight.reshape(1, -1),
+                jnp.broadcast_to(ridge.reshape(1, 1), (1, LANES)),
+            )
+        )
     )
 
 
@@ -554,21 +579,12 @@
 
 
 def finish_kernel(
-    norm_scale, coupled_hbm, matrix_hbm, q_ref, r_head_ref, r_hbm, reduced_hbm,
-    coupled, matrix, r_out, reduced_out, in_sem, out_sem,
+    norm_scale, coupled, matrix, q_ref, r_head_ref, r_hbm, reduced_hbm,
+    r_out, reduced_out, out_sem,
 ):
     units, _, owners, _, _ = coupled.shape
     unit_cols = matrix.shape[2]
     width = unit_cols // owners
-    loads = []
-    for u in range(units):
-        pair = (
-            pltpu.make_async_copy(coupled_hbm.at[u], coupled.at[u], in_sem.at[0, u]),
-            pltpu.make_async_copy(matrix_hbm.at[u], matrix.at[u], in_sem.at[1, u]),
-        )
-        for load in pair:
-            load.start()
-        loads.append(pair)
     q_cols = q_ref[...]
     q_high, q_low = split_bf16(q_cols)
     q_wide = jnp.concatenate([q_high, q_low], axis=1)
@@ -576,8 +592,6 @@
     part = unit_cols // PARTS
     stores = []
     for u in range(units):
-        for load in loads[u]:
-            load.wait()
         for h in range(PARTS):
             mine = range(h * owners // PARTS, (h + 1) * owners // PARTS)
             block = jnp.concatenate(
@@ -610,7 +624,7 @@
     units = coupled.shape[0]
     _, eq_count, unit_cols = matrix.shape
     vmem = pl.BlockSpec(memory_space=pltpu.VMEM)
-    hbm = pl.BlockSpec(memory_space=pl.ANY)
+    hbm = pl.BlockSpec(memory_space=pltpu.HBM)
     r_shape = (WIDE, units * unit_cols)
     reduced_shape = (eq_count, units * unit_cols)
     return pl.pallas_call(
@@ -619,16 +633,14 @@
             jax.ShapeDtypeStruct(r_shape, F32),
             jax.ShapeDtypeStruct(reduced_shape, F32),
         ),
-        in_specs=[hbm, hbm, vmem, vmem],
+        in_specs=[vmem] * 4,
         out_specs=(hbm, hbm),
         scratch_shapes=[
-            pltpu.VMEM(coupled.shape, BF16),
-            pltpu.VMEM(matrix.shape, F32),
             pltpu.VMEM(r_shape, F32),
             pltpu.VMEM(reduced_shape, F32),
-            pltpu.SemaphoreType.DMA((2, units)),
             pltpu.SemaphoreType.DMA((2, units * PARTS)),
         ],
+        compiler_params=pltpu.CompilerParams(vmem_limit_bytes=FINISH_VMEM),
     )(coupled, matrix, q_cols, r_head)
 
 

time: 61.5 us -> 57.6 us (0.937)
  Pallas kernels: 60 us -> 55.7 us
    pallas_call x1, Pallas kernels: 56.1 us -> 53.8 us  [fit(): pl.pallas_call(functools.partial(fit_kernel, owners, cores, units, groups...]
    pallas_call x1, Pallas kernels: 3.89 us -> 1.82 us  [finish(): pl.pallas_call(functools.partial(finish_kernel, norm_scale), out_shape=(j...]
where the time goes in v5:
time: 57.6 us; the launch traced here: 57.5 us
  Pallas kernels  55.7 us (97%)
  between operations  1.28 us (2%)
    pallas_call x1, Pallas kernels, fit(): pl.pallas_call(functools.partial(fit_kernel, owners, cores, units, groups...  53.8 us
    pallas_call x1, Pallas kernels, finish(): pl.pallas_call(functools.partial(finish_kernel, norm_scale), out_shape=(j...  1.82 us

profile of v5, /device:TPU:0, one launch (start us, length us, event | category | flops | bytes accessed | tf_op | source)
XLA Modules:
  0.0 57.5 jit_solution(11296365561886910347)
XLA Ops:
  1.3 0.5 broadcast_in_dim.8.ridge_hbm
  1.8 53.8 %shard_map.86 = (bf16[2,2,16,64,128]{4,3,2,1,0:T(8,128)(2,1)S(1)}, f32[2,64,2048]{2,1,0:T(8,128)S(1)}, f32[64,128]{1,0:T(8,128)S(1)}, f32[128,128]{1,0:T(8,128)S(1)}) custom-call(bf16[128,1024]{1,0:T(8,128)(2,1)} %desc_hbm.1, s32[1,256]{1,0:T(1,128)} %bitcast.7, s32[1,256]{1,0:T(1,128)} %bitcast.8, bf16[4096,1024]{1,0:T(8,128)(2,1)} %points_hbm.1, ...), custom_call_target="tpu_custom_call" | custom-call | tf_op jit(solution)/shard_map/pallas_call | solution.py:511
  55.6 1.8 %shard_map.87 = (f32[128,4096]{1,0:T(8,128)}, f32[64,4096]{1,0:T(8,128)}) custom-call(bf16[2,2,16,64,128]{4,3,2,1,0:T(8,128)(2,1)S(1)} %get-tuple-element.6.coupled, f32[2,64,2048]{2,1,0:T(8,128)S(1)} %get-tuple-element.7.matrix, f32[64,128]{1,0:T(8,128)S(1)} %get-tuple-element.8.q_ref, f32[128,128]{1,0:T(8,128)S(1)} %get-tuple-element.9.r_head_ref), custom_call_target="tpu_custom_call" | custom-call | tf_op jit(solution)/shard_map/pallas_call | solution.py:630

commit v6 on v5

--- a/solution.py
+++ b/solution.py
@@ -399,26 +399,31 @@
             (bit_of(me, bit(u, i)) * (owners >> (i + 1)) for i in range(t)), jnp.int32(0)
         )
 
-    def quarter_copy(u, k, t, second):
-        quarter = owners // 4
-        own = bit_of(me, bit(u, 1))
-        at = start_of(u, 1) + (1 - own if second else own) * quarter
-        part = whole.at[u, k, pl.ds(at, quarter)]
-        to = me + (1 - 2 * bit_of(me, bit(u, t))) * (1 << bit(u, t))
-        index = 2 * t + second
+    def peer(u, t):
+        return me + (1 - 2 * bit_of(me, bit(u, t))) * (1 << bit(u, t))
+
+    def piece_copy(u, k, t, slot):
+        part = whole.at[u, k, start_of(u, 2) + slot]
+        index = 1 + (1 + t) * line + slot
         return pltpu.make_async_remote_copy(
             src_ref=part, dst_ref=part, send_sem=r_send.at[u, k, index],
-            recv_sem=r_recv.at[u, k, index], device_id={"rows": to}, device_id_type=MESH,
-        )
-
-    def gather_copy(u, k, index):
-        return quarter_copy(u, k, (0, 0, 1)[index], (False, True, False)[index])
+            recv_sem=r_recv.at[u, k, index], device_id={"rows": peer(u, t)}, device_id_type=MESH,
+        )
+
+    def quarter_copy(u, k):
+        quarter = owners // 4
+        at = start_of(u, 1) + (1 - bit_of(me, bit(u, 1))) * quarter
+        part = whole.at[u, k, pl.ds(at, quarter)]
+        return pltpu.make_async_remote_copy(
+            src_ref=part, dst_ref=part, send_sem=r_send.at[u, k, 0],
+            recv_sem=r_recv.at[u, k, 0], device_id={"rows": peer(u, 0)}, device_id_type=MESH,
+        )
 
     def line_copy(u, k, to, sender):
         part = whole.at[u, k, start_of(u, 2) + sender]
         return pltpu.make_async_remote_copy(
-            src_ref=part, dst_ref=part, send_sem=r_send.at[u, k, 3 + to],
-            recv_sem=r_recv.at[u, k, 3 + sender],
+            src_ref=part, dst_ref=part, send_sem=r_send.at[u, k, 1 + to],
+            recv_sem=r_recv.at[u, k, 1 + sender],
             device_id={"rows": to * 4 + me % 4}, device_id_type=MESH,
         )
 
@@ -428,6 +433,8 @@
         whole[u, k, start_of(u, 2) + rank] = value.astype(BF16)
         for to in others:
             line_copy(u, k, to, rank).start()
+        for t in (1, 0):
+            piece_copy(u, k, t, rank).start()
 
     def open_unit(u):
         lax.fori_loop(1, owners, blocks[u], 0)
@@ -442,18 +449,20 @@
         for k in range(PANELS):
             for other in others:
                 line_copy(u, k, other, other).wait_recv()
-            gather_copy(u, k, 2).start()
-            gather_copy(u, k, 0).start()
+                for t in (1, 0):
+                    piece_copy(u, k, t, other).start()
 
     def middle(u):
         for k in range(PANELS):
-            gather_copy(u, k, 2).wait_recv()
-            gather_copy(u, k, 1).start()
+            for slot in range(line):
+                piece_copy(u, k, 1, slot).wait_recv()
+            quarter_copy(u, k).start()
 
     def last(u):
         for k in range(PANELS):
-            gather_copy(u, k, 0).wait_recv()
-            gather_copy(u, k, 1).wait_recv()
+            for slot in range(line):
+                piece_copy(u, k, 0, slot).wait_recv()
+            quarter_copy(u, k).wait_recv()
         out = pltpu.make_async_copy(whole.at[u], coupled_ref.at[u], out_sem.at[u])
         out.start()
         outs.append(out)
@@ -465,8 +474,10 @@
 
     for u in range(units):
         for k in range(PANELS):
-            for index in range(3):
-                gather_copy(u, k, index).wait_send()
+            for slot in range(line):
+                for t in (1, 0):
+                    piece_copy(u, k, t, slot).wait_send()
+            quarter_copy(u, k).wait_send()
             for to in others:
                 line_copy(u, k, to, rank).wait_send()
     for out in outs:
@@ -553,8 +564,8 @@
             dma((cores, owners)),
             dma((units, owners)),
             dma((units, owners)),
-            dma((units, PANELS, 3 + line)),
-            dma((units, PANELS, 3 + line)),
+            dma((units, PANELS, 1 + 3 * line)),
+            dma((units, PANELS, 1 + 3 * line)),
         ],
         compiler_params=pltpu.CompilerParams(
             collective_id=0, has_side_effects=True, vmem_limit_bytes=FIT_VMEM

time: 57.6 us -> 56.6 us (0.983)
  Pallas kernels: 55.7 us -> 54.6 us
    pallas_call x1, Pallas kernels: 53.8 us -> 52.8 us  [fit(): pl.pallas_call(functools.partial(fit_kernel, owners, cores, units, groups...]
where the time goes in v6:
time: 56.6 us; the launch traced here: 56.4 us
  Pallas kernels  54.6 us (96%)
  between operations  1.28 us (2%)
    pallas_call x1, Pallas kernels, fit(): pl.pallas_call(functools.partial(fit_kernel, owners, cores, units, groups...  52.8 us
    pallas_call x1, Pallas kernels, finish(): pl.pallas_call(functools.partial(finish_kernel, norm_scale), out_shape=(j...  1.82 us

profile of v6, /device:TPU:0, one launch (start us, length us, event | category | flops | bytes accessed | tf_op | source)
XLA Modules:
  0.0 56.4 jit_solution(7459846340204975350)
XLA Ops:
  1.3 0.5 broadcast_in_dim.8.ridge_hbm
  1.8 52.8 %shard_map.86 = (bf16[2,2,16,64,128]{4,3,2,1,0:T(8,128)(2,1)S(1)}, f32[2,64,2048]{2,1,0:T(8,128)S(1)}, f32[64,128]{1,0:T(8,128)S(1)}, f32[128,128]{1,0:T(8,128)S(1)}) custom-call(bf16[128,1024]{1,0:T(8,128)(2,1)} %desc_hbm.1, s32[1,256]{1,0:T(1,128)} %bitcast.7, s32[1,256]{1,0:T(1,128)} %bitcast.8, bf16[4096,1024]{1,0:T(8,128)(2,1)} %points_hbm.1, ...), custom_call_target="tpu_custom_call" | custom-call | tf_op jit(solution)/shard_map/pallas_call | solution.py:522
  54.6 1.8 %shard_map.87 = (f32[128,4096]{1,0:T(8,128)}, f32[64,4096]{1,0:T(8,128)}) custom-call(bf16[2,2,16,64,128]{4,3,2,1,0:T(8,128)(2,1)S(1)} %get-tuple-element.6.coupled, f32[2,64,2048]{2,1,0:T(8,128)S(1)} %get-tuple-element.7.matrix, f32[64,128]{1,0:T(8,128)S(1)} %get-tuple-element.8.q_ref, f32[128,128]{1,0:T(8,128)S(1)} %get-tuple-element.9.r_head_ref), custom_call_target="tpu_custom_call" | custom-call | tf_op jit(solution)/shard_map/pallas_call | solution.py:641
